TPU v7x, 32 devices: a whole 2x2x4 slice. The times are simulated.
32 devices in a mesh: rep: 1, seq: 8 (over z, y), head: 2 (over x), sub: 2 (over core).
Axes of the slice: x: 2, y: 2, z: 4, core: 2. Of those that a mesh axis runs over, the one named last changes fastest.
Arguments:
- head_query_rows: bfloat16 [2048, 2048], P(('rep', 'seq', 'sub'), 'head'), may hold values from -6 to 6, as said below
- head_key_rows: bfloat16 [2048, 2048], P(('rep', 'seq', 'sub'), 'head'), may hold values from -6 to 6, as said below
- head_value_rows: bfloat16 [2048, 2048], P(('rep', 'seq', 'sub'), 'head'), may hold values from -6 to 6
- output_gradient: bfloat16 [2048, 4096], P(('rep', 'seq', 'sub'), 'head'), may hold values from -6 to 6
- output_matrix: bfloat16 [2048, 4096], P('head', 'sub'), may hold values from -0.125 to 0.125
- adapter_down_weight: bfloat16 [2048, 16], P('head'), may hold values from -0.125 to 0.125
- adapter_up_weight: bfloat16 [16, 4096], replicated, may hold values from -0.09375 to 0.09375
Outputs:
- query_gradient: bfloat16 [2048, 2048], P(('rep', 'seq', 'sub'), 'head')
- key_gradient: bfloat16 [2048, 2048], P(('rep', 'seq', 'sub'), 'head')
- value_gradient: bfloat16 [2048, 2048], P(('rep', 'seq', 'sub'), 'head')
- adapter_down_gradient: float32 [2048, 16], P(('rep', 'head'))
- adapter_up_gradient: float32 [16, 4096], P('rep', 'head')
Inputs may be any that keep to these rules, and one draw needn't show every extreme that they name: `head_query_rows`: entries of the queries are real values within the range. `head_key_rows`: entries of the keys are real values within the range.
All inputs are finite; a program needn't handle non-finite values.
Results may differ from a plain program's by a relative error of at most 0.029.
Values may be sent and summed in bfloat16 or wider, within the bound.
A program may use at most 64 MiB of HBM per device.

v0:
```python
import jax
import jax.numpy as jnp
from jax import lax
from jax.sharding import PartitionSpec as P

HD = 128
GROUP = 2048


def passed_along(value, axis, by):
    peers = lax.axis_size(axis)
    return lax.ppermute(value, axis, [(i, (i + by) % peers) for i in range(peers)])


def placed_visible(row_count, window_rows, seq_total, first_row, back_rows, roll_by):
    query_pos = first_row + lax.broadcasted_iota(jnp.int32, (row_count, window_rows), 0)
    key_pos = (
        first_row
        - back_rows
        + seq_total
        + lax.broadcasted_iota(jnp.int32, (row_count, window_rows), 1)
    ) % seq_total
    query_order = (query_pos - roll_by + seq_total) % seq_total
    key_order = (key_pos - roll_by + seq_total) % seq_total
    return (query_order // GROUP == key_order // GROUP) & (key_order <= query_order)


def softmax_rows(query_head, keys_head, visible):
    scores = lax.dot_general(
        query_head, keys_head, (((1,), (1,)), ((), ())), preferred_element_type=jnp.float32
    )
    scores = jnp.where(visible, scores * HD ** (-0.5), -jnp.inf)
    highest = jnp.max(scores, axis=1, keepdims=True)
    powers = jnp.exp(scores - highest)
    return powers / jnp.sum(powers, axis=1, keepdims=True)


def head_forward(query_head, window_head, visible):
    prob = softmax_rows(query_head, window_head[0], visible)
    return jnp.dot(
        prob.astype(jnp.bfloat16), window_head[1], preferred_element_type=jnp.float32
    ).astype(jnp.bfloat16)


def head_backward(query_head, window_head, dout_head, visible):
    prob = softmax_rows(query_head, window_head[0], visible)
    prob_lo = prob.astype(jnp.bfloat16)
    dprob = lax.dot_general(
        dout_head, window_head[1], (((1,), (1,)), ((), ())), preferred_element_type=jnp.float32
    )
    delta = jnp.sum(prob * dprob, axis=1, keepdims=True)
    dscore = (prob * (dprob - delta) * HD ** (-0.5)).astype(jnp.bfloat16)
    grad_q = jnp.dot(dscore, window_head[0], preferred_element_type=jnp.float32).astype(
        jnp.bfloat16
    )
    grad_k = lax.dot_general(
        dscore, query_head, (((0,), (0,)), ((), ())), preferred_element_type=jnp.float32
    )
    grad_v = lax.dot_general(
        prob_lo, dout_head, (((0,), (0,)), ((), ())), preferred_element_type=jnp.float32
    )
    return (grad_q, jnp.stack((grad_k.astype(jnp.bfloat16), grad_v.astype(jnp.bfloat16))))


def attend_window(query_rows, window, dout_rows, visible):
    row_count, feat_count = query_rows.shape
    heads_here = feat_count // HD
    window_rows = window.shape[1]
    window_heads = window.reshape(2, window_rows, heads_here, HD).transpose(2, 0, 1, 3)
    query_heads = query_rows.reshape(row_count, heads_here, HD).transpose(1, 0, 2)
    dout_heads = dout_rows.reshape(row_count, heads_here, HD).transpose(1, 0, 2)
    attn_heads = lax.map(
        lambda pieces: head_forward(pieces[0], pieces[1], visible), (query_heads, window_heads)
    )
    grad_q_heads, pair_heads = lax.map(
        lambda pieces: head_backward(pieces[0], pieces[1], pieces[2], visible),
        (query_heads, window_heads, dout_heads),
    )
    attention_output = attn_heads.transpose(1, 0, 2).reshape(row_count, feat_count)
    query_gradient = grad_q_heads.transpose(1, 0, 2).reshape(row_count, feat_count)
    pair_grads = pair_heads.transpose(1, 2, 0, 3).reshape(2, window_rows, feat_count)
    return (attention_output, query_gradient, pair_grads)


def on_device(
    head_query_rows,
    head_key_rows,
    head_value_rows,
    output_gradient,
    output_matrix,
    adapter_down_weight,
    adapter_up_weight,
):
    tokens_dev, feat_dev = head_query_rows.shape
    head_index = lax.axis_index("head")
    shifted = head_index >= lax.axis_size("head") // 2
    total_gradient = lax.all_gather(output_gradient, "head", axis=1, tiled=True)
    projected_output = lax.dot_general(
        total_gradient,
        lax.all_gather(output_matrix, "sub", axis=1, tiled=True),
        (((1,), (1,)), ((), ())),
        preferred_element_type=jnp.float32,
    )
    adapter_upward = lax.dot_general(
        total_gradient,
        adapter_up_weight,
        (((1,), (1,)), ((), ())),
        preferred_element_type=jnp.float32,
    )
    adapter_backward = jnp.dot(
        adapter_upward, adapter_down_weight.astype(jnp.float32).T, precision=lax.Precision.HIGHEST
    )
    attention_gradient = (projected_output + 2.0 * adapter_backward).astype(jnp.bfloat16)
    sub_count = lax.axis_size("sub")
    block_rows = tokens_dev * sub_count
    seq_total = block_rows * lax.axis_size("seq")
    reach = max(GROUP // block_rows - 1, 1)
    roll_by = jnp.where(shifted, GROUP // 2, 0)
    stacked = jnp.stack((head_query_rows, head_key_rows, head_value_rows, attention_gradient))
    moved = lax.all_to_all(stacked, "sub", split_axis=2, concat_axis=1, tiled=True)
    own_pair = moved[1:3]
    received = [passed_along(own_pair, "seq", distance) for distance in range(reach, 0, -1)]
    window = jnp.concatenate(received + [own_pair], axis=1)
    first_row = lax.axis_index("seq") * block_rows
    visible = placed_visible(
        block_rows, window.shape[1], seq_total, first_row, reach * block_rows, roll_by
    )
    attn_local, grad_q_local, pair_grads = attend_window(moved[0], window, moved[3], visible)
    running = pair_grads[:, reach * block_rows :].astype(jnp.float32)
    for distance in range(1, reach + 1):
        begin_row = (reach - distance) * block_rows
        block_terms = pair_grads[:, begin_row : begin_row + block_rows]
        returned = passed_along(block_terms, "seq", -distance)
        running = running + returned.astype(jnp.float32)
    pair_local = running.astype(jnp.bfloat16)
    back = jnp.stack((attn_local, grad_q_local, pair_local[0], pair_local[1]))
    restored = lax.all_to_all(back, "sub", split_axis=1, concat_axis=2, tiled=True)
    attention_output = restored[0]
    query_gradient = restored[1]
    key_gradient = restored[2]
    value_gradient = restored[3]
    middle_piece = jnp.dot(
        attention_output, adapter_down_weight, preferred_element_type=jnp.float32
    )
    down_gradient_part = 2.0 * jnp.dot(
        attention_output.astype(jnp.float32).T, adapter_upward, precision=lax.Precision.HIGHEST
    )
    adapter_middle = lax.psum(middle_piece, "head")
    up_gradient_part = 2.0 * jnp.dot(
        adapter_middle.T, output_gradient.astype(jnp.float32), precision=lax.Precision.HIGHEST
    )
    adapter_down_gradient, adapter_up_gradient = lax.psum(
        (down_gradient_part, up_gradient_part), ("seq", "sub")
    )
    return (
        query_gradient,
        key_gradient,
        value_gradient,
        adapter_down_gradient,
        adapter_up_gradient,
    )


def solution(mesh):
    in_specs = (
        P(("rep", "seq", "sub"), "head"),
        P(("rep", "seq", "sub"), "head"),
        P(("rep", "seq", "sub"), "head"),
        P(("rep", "seq", "sub"), "head"),
        P("head", "sub"),
        P("head", None),
        P(),
    )
    out_specs = (
        P(("rep", "seq", "sub"), "head"),
        P(("rep", "seq", "sub"), "head"),
        P(("rep", "seq", "sub"), "head"),
        P(("rep", "head"), None),
        P("rep", "head"),
    )
    return jax.shard_map(
        on_device, mesh=mesh, in_specs=in_specs, out_specs=out_specs, check_vma=False
    )
```

profile of v0, /device:TPU:1, one launch (start us, length us, event | category | flops | bytes accessed | tf_op | source)
XLA Modules:
  0.0 432.9 jit_solution(16442148612122126601)
XLA Ops:
  8.7 24.3 %all-gather.3.cloned.1.call-done = bf16[128,4096]{1,0:T(8,128)(2,1)} async-done(((bf16[128,2048]{1,0:T(8,128)(2,1)}), bf16[128,4096]{1,0:T(8,128)(2,1)}) %all-gather.3.cloned.1.call-update) | async-done | bytes 1048592 | tf_op jit(solution)/shard_map/all_gather | solution.py:97
  34.6 20.2 %all-gather.5.cloned.1.call-done = bf16[1024,4096]{1,0:T(8,128)(2,1)} async-done(((bf16[1024,2048]{1,0:T(8,128)(2,1)}), bf16[1024,4096]{1,0:T(8,128)(2,1)}) %all-gather.5.cloned.1.call-update) | async-done | bytes 8388624 | tf_op jit(solution)/shard_map/all_gather | solution.py:100
  54.8 6.6 %fusion.63 = f32[128,1024]{1,0:T(8,128)S(1)} fusion(bf16[128,4096]{1,0:T(8,128)(2,1)} %all-gather.3.cloned.1.call-done, bf16[1024,4096]{1,0:T(8,128)(2,1)} %all-gather.5.cloned.1.call-done), kind=kOutput, calls=%fused_computation.133 | convolution fusion | flops 1073741824 | bytes 9961472 | tf_op jit(solution)/shard_map/dot_general | solution.py:98
  62.8 4.5 %all_to_all.30 = bf16[4,128,1024]{1,0,2:T(4,128)(2,1)S(1)} all-to-all(bf16[4,128,1024]{1,0,2:T(4,128)(2,1)S(1)} %copy.81), channel_id=1, replica_groups=mesh['rep'=1,'seq'=8,'head'=2,'sub'=2] {'sub'}, dimensions={2} | all-to-all | bytes 2097152 | tf_op jit(solution)/shard_map/all_to_all | solution.py:120
  67.7 4.3 collective-permute-start
  73.5 2.4 collective-permute-start.3
  75.9 7.1 %collective-permute-done = bf16[2,256,512]{2,1,0:T(8,128)(2,1)S(1)} collective-permute-done((bf16[2,256,512]{2,1,0:T(8,128)(2,1)S(1)}, bf16[2,256,512]{2,1,0:T(8,128)(2,1)S(1)}, u32[]{:S(2)}, u32[]{:S(2)}) %collective-permute-start) | collective-permute-done | bytes 524320 | tf_op jit(solution)/shard_map/ppermute | solution.py:12
  86.2 8.0 %collective-permute-done.1 = bf16[2,256,512]{2,1,0:T(8,128)(2,1)} collective-permute-done((bf16[2,256,512]{2,1,0:T(8,128)(2,1)S(1)}, bf16[2,256,512]{2,1,0:T(8,128)(2,1)}, u32[]{:S(2)}, u32[]{:S(2)}) %collective-permute-start.1) | collective-permute-done | bytes 524320 | tf_op jit(solution)/shard_map/ppermute | solution.py:12
  97.2 8.3 %collective-permute-done.2 = bf16[2,256,512]{2,1,0:T(8,128)(2,1)} collective-permute-done((bf16[2,256,512]{2,1,0:T(8,128)(2,1)S(1)}, bf16[2,256,512]{2,1,0:T(8,128)(2,1)}, u32[]{:S(2)}, u32[]{:S(2)}) %collective-permute-start.2) | collective-permute-done | bytes 524320 | tf_op jit(solution)/shard_map/ppermute | solution.py:12
  106.8 55.0 %collective-permute-done.3 = bf16[2,256,512]{2,1,0:T(8,128)(2,1)} collective-permute-done((bf16[2,256,512]{2,1,0:T(8,128)(2,1)S(1)}, bf16[2,256,512]{2,1,0:T(8,128)(2,1)}, u32[]{:S(2)}, u32[]{:S(2)}) %collective-permute-start.3) | collective-permute-done | bytes 524320 | tf_op jit(solution)/shard_map/ppermute | solution.py:12
  172.1 6.2 %copy.95 = bf16[4,2,2048,128]{3,2,1,0:T(8,128)(2,1)} copy(bf16[4,2,2048,128]{2,3,0,1:T(8,128)(2,1)} %bitcast.16) | data formatting | bytes 8388608
  179.0 42.9 %while.25 = (s32[]{:T(128)}, bf16[4,256,128]{1,2,0:T(8,128)(2,1)}, bf16[4,2,2048,128]{2,3,0,1:T(8,128)(2,1)}, bf16[4,256,128]{2,1,0:T(8,128)(2,1)S(1)}, bf16[4,2...) while((s32[]{:T(128)}, bf16[4,256,128]{1,2,0:T(8,128)(2,1)}, ...), condition=%wide.region_8.9_spmd.clone, body=%wide.region_4.8_spmd.clone.sunk | while | flops 706772224 | bytes 27380468 | solution.py:75
  179.0 1.9 fusion.101
  189.7 1.9 fusion.101
  200.4 1.9 fusion.101
  211.1 1.9 fusion.101
  221.9 3.5 fusion.60
  225.3 2.4 collective-permute-start.11
  227.8 2.0 collective-permute-start.10
  230.1 10.2 %collective-permute-done.13 = bf16[2,256,512]{1,2,0:T(8,128)(2,1)S(1)} collective-permute-done((bf16[2,256,512]{1,2,0:T(8,128)(2,1)S(1)}, bf16[2,256,512]{1,2,0:T(8,128)(2,1)S(1)}, u32[]{:S(2)}, u32[]{:S(2)}) %collective-permute-start.13) | collective-permute-done | bytes 524320 | tf_op jit(solution)/shard_map/ppermute | solution.py:12
  240.4 10.5 %collective-permute-start.7 = (bf16[2,256,512]{1,2,0:T(8,128)(2,1)S(1)}, bf16[2,256,512]{1,2,0:T(8,128)(2,1)}, u32[]{:S(2)}, u32[]{:S(2)}) collective-permute-start(bf16[2,256,512]{1,2,0:T(8,128)(2,1)S(1)} %get-tuple-element.306), channel_id=1, source_target_pairs={{0,28},{4,0},{8,4},{12,8},{16,12},{20,16},{24,20},{28,24},{1,29},{... | collective-permute-start | bytes 1572872 | tf_op jit(solution)/shard_map/ppermute | solution.py:12
  250.9 16.3 %while.24 = (s32[]{:T(128)}, bf16[4,256,128]{1,2,0:T(8,128)(2,1)S(1)}, bf16[4,256,128]{2,1,0:T(8,128)(2,1)S(1)}, bf16[4,2,2048,128]{3,2,1,0:T(8,128)(2,1)}, s32[...) while((s32[]{:T(128)}, ...), condition=%wide.region_3.4_spmd.clone, body=%wide.region_0.3_spmd.clone.sunk | while | flops 297827840 | bytes 7761061 | solution.py:72
  250.9 1.9 fusion.93
  255.0 1.9 fusion.93
  259.1 1.9 fusion.93
  263.1 1.9 fusion.93
  267.2 19.7 %collective-permute-done.11 = bf16[2,256,512]{1,2,0:T(8,128)(2,1)} collective-permute-done((bf16[2,256,512]{1,2,0:T(8,128)(2,1)}, bf16[2,256,512]{1,2,0:T(8,128)(2,1)}, u32[]{:S(2)}, u32[]{:S(2)}) %collective-permute-start.11) | collective-permute-done | bytes 524320 | tf_op jit(solution)/shard_map/ppermute | solution.py:12
  287.0 4.9 %collective-permute-done.7 = bf16[2,256,512]{1,2,0:T(8,128)(2,1)} collective-permute-done((bf16[2,256,512]{1,2,0:T(8,128)(2,1)S(1)}, bf16[2,256,512]{1,2,0:T(8,128)(2,1)}, u32[]{:S(2)}, u32[]{:S(2)}) %collective-permute-start.7) | collective-permute-done | bytes 524320 | tf_op jit(solution)/shard_map/ppermute | solution.py:12
  291.9 2.7 add_convert_fusion
  295.7 6.0 %all_to_all.31 = bf16[4,256,512]{2,0,1:T(4,128)(2,1)S(1)} all-to-all(bf16[4,256,512]{2,0,1:T(4,128)(2,1)S(1)} %copy.103), channel_id=1, replica_groups=mesh['rep'=1,'seq'=8,'head'=2,'sub'=2] {'sub'}, dimensions={1} | all-to-all | bytes 2097152 | tf_op jit(solution)/shard_map/all_to_all | solution.py:137
  303.5 4.0 psum.22
  311.6 111.7 %all-reduce.3.cloned.1.call-done = (f32[1024,16]{0,1:T(8,128)}, f32[16,2048]{1,0:T(8,128)}) async-done(((f32[1024,16]{0,1:T(8,128)}, f32[16,2048]{1,0:T(8,128)}), (f32[1024,16]{0,1:T(8,128)}, f32[16,2048]{1,0:T(8,128)})) %all-reduce.3.cloned.1.call-update) | async-done | bytes 196624 | tf_op jit(solution)/shard_map/psum | solution.py:152
  (182 shorter events, 79.0 us)
Async XLA Ops:
  7.2 25.8 %copy-start = (bf16[16,4096]{1,0:T(8,128)(2,1)S(1)}, bf16[16,4096]{1,0:T(8,128)(2,1)}, u32[]{:S(2)}) copy-start(bf16[16,4096]{1,0:T(8,128)(2,1)} %param.17) | copy-start | bytes 393220
  7.2 25.8 %all-gather.3.cloned.1.call-start = ((), (), s32[]{:S(2)}) async-start(), calls=%async_computation.2 | async-start | bytes 1572864 | tf_op jit(solution)/shard_map/all_gather | solution.py:97
  7.9 46.9 %all-gather.5.cloned.1.call-start = ((), (), s32[]{:S(2)}) async-start(), calls=%async_computation.3 | async-start | bytes 12582912 | tf_op jit(solution)/shard_map/all_gather | solution.py:100
  8.7 414.7 %all-reduce.3.cloned.1.call-start = ((), (), s32[]{:S(2)}) async-start(), calls=%async_computation.4 | async-start | bytes 393216 | tf_op jit(solution)/shard_map/psum | solution.py:152
  34.6 26.8 %copy-start.13 = (f32[128,16]{0,1:T(8,128)}, f32[128,16]{0,1:T(8,128)S(1)}, u32[]{:S(2)}) copy-start(f32[128,16]{0,1:T(8,128)S(1)} %fusion.64) | copy-start | bytes 24580
  34.6 26.8 %copy-start.11 = (bf16[1024,16]{0,1:T(8,128)(2,1)S(1)}, bf16[1024,16]{0,1:T(8,128)(2,1)}, u32[]{:S(2)}) copy-start(bf16[1024,16]{0,1:T(8,128)(2,1)} %param.16) | copy-start | bytes 98308
  34.6 27.3 %copy-start.8 = (bf16[128,1024]{1,0:T(8,128)(2,1)S(1)}, bf16[128,1024]{1,0:T(8,128)(2,1)}, u32[]{:S(2)}) copy-start(bf16[128,1024]{1,0:T(8,128)(2,1)} %param.13) | copy-start | bytes 786436
  34.6 27.3 %copy-start.9 = (bf16[128,1024]{1,0:T(8,128)(2,1)S(1)}, bf16[128,1024]{1,0:T(8,128)(2,1)}, u32[]{:S(2)}) copy-start(bf16[128,1024]{1,0:T(8,128)(2,1)} %param.12) | copy-start | bytes 786436
  34.6 27.3 %copy-start.10 = (bf16[128,1024]{1,0:T(8,128)(2,1)S(1)}, bf16[128,1024]{1,0:T(8,128)(2,1)}, u32[]{:S(2)}) copy-start(bf16[128,1024]{1,0:T(8,128)(2,1)} %param.11) | copy-start | bytes 786436
  67.7 15.3 %collective-permute-start = (bf16[2,256,512]{2,1,0:T(8,128)(2,1)S(1)}, bf16[2,256,512]{2,1,0:T(8,128)(2,1)S(1)}, u32[]{:S(2)}, u32[]{:S(2)}) collective-permute-start(bf16[2,256,512]{2,1,0:T(8,128)(2,1)S(1)} %bitcast.158), channel_id=1, source_target_pairs={{0,28},{4,0},{8,4},{12,8},{16,12},{20,16},{24,20},{28,24},{1,29},{... | collective-permute-start | bytes 1572872 | tf_op jit(solution)/shard_map/ppermute | solution.py:12
  72.0 22.2 %collective-permute-start.1 = (bf16[2,256,512]{2,1,0:T(8,128)(2,1)S(1)}, bf16[2,256,512]{2,1,0:T(8,128)(2,1)}, u32[]{:S(2)}, u32[]{:S(2)}) collective-permute-start(bf16[2,256,512]{2,1,0:T(8,128)(2,1)S(1)} %bitcast.159), channel_id=1, source_target_pairs={{0,24},{4,28},{8,0},{12,4},{16,8},{20,12},{24,16},{28,20},{1,25},{... | collective-permute-start | bytes 1572872 | tf_op jit(solution)/shard_map/ppermute | solution.py:12
  73.5 32.0 %collective-permute-start.2 = (bf16[2,256,512]{2,1,0:T(8,128)(2,1)S(1)}, bf16[2,256,512]{2,1,0:T(8,128)(2,1)}, u32[]{:S(2)}, u32[]{:S(2)}) collective-permute-start(bf16[2,256,512]{2,1,0:T(8,128)(2,1)S(1)} %bitcast.160), channel_id=1, source_target_pairs={{0,20},{4,24},{8,28},{12,0},{16,4},{20,8},{24,12},{28,16},{1,21},{... | collective-permute-start | bytes 1572872 | tf_op jit(solution)/shard_map/ppermute | solution.py:12
  73.5 88.2 %collective-permute-start.3 = (bf16[2,256,512]{2,1,0:T(8,128)(2,1)S(1)}, bf16[2,256,512]{2,1,0:T(8,128)(2,1)}, u32[]{:S(2)}, u32[]{:S(2)}) collective-permute-start(bf16[2,256,512]{2,1,0:T(8,128)(2,1)S(1)} %bitcast.161), channel_id=1, source_target_pairs={{0,16},{4,20},{8,24},{12,28},{16,0},{20,4},{24,8},{28,12},{1,17},{... | collective-permute-start | bytes 1572872 | tf_op jit(solution)/shard_map/ppermute | solution.py:12
  75.9 87.1 %collective-permute-start.4 = (bf16[2,256,512]{2,1,0:T(8,128)(2,1)S(1)}, bf16[2,256,512]{2,1,0:T(8,128)(2,1)}, u32[]{:S(2)}, u32[]{:S(2)}) collective-permute-start(bf16[2,256,512]{2,1,0:T(8,128)(2,1)S(1)} %bitcast.162), channel_id=1, source_target_pairs={{0,12},{4,16},{8,20},{12,24},{16,28},{20,0},{24,4},{28,8},{1,13},{... | collective-permute-start | bytes 1572872 | tf_op jit(solution)/shard_map/ppermute | solution.py:12
  83.0 81.2 %collective-permute-start.5 = (bf16[2,256,512]{2,1,0:T(8,128)(2,1)S(1)}, bf16[2,256,512]{2,1,0:T(8,128)(2,1)}, u32[]{:S(2)}, u32[]{:S(2)}) collective-permute-start(bf16[2,256,512]{2,1,0:T(8,128)(2,1)S(1)} %bitcast.163), channel_id=1, source_target_pairs={{0,8},{4,12},{8,16},{12,20},{16,24},{20,28},{24,0},{28,4},{1,9},{5... | collective-permute-start | bytes 1572872 | tf_op jit(solution)/shard_map/ppermute | solution.py:12
  94.2 74.8 %collective-permute-start.6 = (bf16[2,256,512]{2,1,0:T(8,128)(2,1)S(1)}, bf16[2,256,512]{2,1,0:T(8,128)(2,1)}, u32[]{:S(2)}, u32[]{:S(2)}) collective-permute-start(bf16[2,256,512]{2,1,0:T(8,128)(2,1)S(1)} %bitcast.164), channel_id=1, source_target_pairs={{0,4},{4,8},{8,12},{12,16},{16,20},{20,24},{24,28},{28,0},{1,5},{5... | collective-permute-start | bytes 1572872 | tf_op jit(solution)/shard_map/ppermute | solution.py:12
  179.0 1.9 copy-start.15
  189.7 1.9 copy-start.15
  200.4 1.9 copy-start.15
  211.1 1.9 copy-start.15
  225.3 15.0 %collective-permute-start.13 = (bf16[2,256,512]{1,2,0:T(8,128)(2,1)S(1)}, bf16[2,256,512]{1,2,0:T(8,128)(2,1)S(1)}, u32[]{:S(2)}, u32[]{:S(2)}) collective-permute-start(bf16[2,256,512]{1,2,0:T(8,128)(2,1)S(1)} %get-tuple-element.307), channel_id=1, source_target_pairs={{0,4},{4,8},{8,12},{12,16},{16,20},{20,24},{24,28},{28,0},{1,5},{5... | collective-permute-start | bytes 1572872 | tf_op jit(solution)/shard_map/ppermute | solution.py:12
  225.3 15.0 %collective-permute-start.12 = (bf16[2,256,512]{1,2,0:T(8,128)(2,1)S(1)}, bf16[2,256,512]{1,2,0:T(8,128)(2,1)S(1)}, u32[]{:S(2)}, u32[]{:S(2)}) collective-permute-start(bf16[2,256,512]{1,2,0:T(8,128)(2,1)S(1)} %get-tuple-element.308), channel_id=1, source_target_pairs={{0,8},{4,12},{8,16},{12,20},{16,24},{20,28},{24,0},{28,4},{1,9},{5... | collective-permute-start | bytes 1572872 | tf_op jit(solution)/shard_map/ppermute | solution.py:12
  225.3 61.6 %collective-permute-start.11 = (bf16[2,256,512]{1,2,0:T(8,128)(2,1)}, bf16[2,256,512]{1,2,0:T(8,128)(2,1)}, u32[]{:S(2)}, u32[]{:S(2)}) collective-permute-start(bf16[2,256,512]{1,2,0:T(8,128)(2,1)} %get-tuple-element.309), channel_id=1, source_target_pairs={{0,12},{4,16},{8,20},{12,24},{16,28},{20,0},{24,4},{28,8},{1,13},{... | collective-permute-start | bytes 1572872 | tf_op jit(solution)/shard_map/ppermute | solution.py:12
  227.8 59.2 %collective-permute-start.10 = (bf16[2,256,512]{1,2,0:T(8,128)(2,1)}, bf16[2,256,512]{1,2,0:T(8,128)(2,1)}, u32[]{:S(2)}, u32[]{:S(2)}) collective-permute-start(bf16[2,256,512]{1,2,0:T(8,128)(2,1)} %get-tuple-element.310), channel_id=1, source_target_pairs={{0,16},{4,20},{8,24},{12,28},{16,0},{20,4},{24,8},{28,12},{1,17},{... | collective-permute-start | bytes 1572872 | tf_op jit(solution)/shard_map/ppermute | solution.py:12
  229.8 57.2 %collective-permute-start.9 = (bf16[2,256,512]{1,2,0:T(8,128)(2,1)}, bf16[2,256,512]{1,2,0:T(8,128)(2,1)}, u32[]{:S(2)}, u32[]{:S(2)}) collective-permute-start(bf16[2,256,512]{1,2,0:T(8,128)(2,1)} %get-tuple-element.311), channel_id=1, source_target_pairs={{0,20},{4,24},{8,28},{12,0},{16,4},{20,8},{24,12},{28,16},{1,21},{... | collective-permute-start | bytes 1572872 | tf_op jit(solution)/shard_map/ppermute | solution.py:12
  240.3 10.5 %copy-start.4 = (bf16[2,256,512]{1,2,0:T(8,128)(2,1)}, bf16[2,256,512]{1,2,0:T(8,128)(2,1)S(1)}, u32[]{:S(2)}) copy-start(bf16[2,256,512]{1,2,0:T(8,128)(2,1)S(1)} %collective-permute-done.13) | copy-start | bytes 1572868
  240.3 46.6 %collective-permute-start.8 = (bf16[2,256,512]{1,2,0:T(8,128)(2,1)}, bf16[2,256,512]{1,2,0:T(8,128)(2,1)}, u32[]{:S(2)}, u32[]{:S(2)}) collective-permute-start(bf16[2,256,512]{1,2,0:T(8,128)(2,1)} %get-tuple-element.312), channel_id=1, source_target_pairs={{0,24},{4,28},{8,0},{12,4},{16,8},{20,12},{24,16},{28,20},{1,25},{... | collective-permute-start | bytes 1572872 | tf_op jit(solution)/shard_map/ppermute | solution.py:12
  240.3 10.5 %copy-start.5 = (bf16[2,256,512]{1,2,0:T(8,128)(2,1)}, bf16[2,256,512]{1,2,0:T(8,128)(2,1)S(1)}, u32[]{:S(2)}) copy-start(bf16[2,256,512]{1,2,0:T(8,128)(2,1)S(1)} %collective-permute-done.12) | copy-start | bytes 1572868
  240.4 51.5 %collective-permute-start.7 = (bf16[2,256,512]{1,2,0:T(8,128)(2,1)S(1)}, bf16[2,256,512]{1,2,0:T(8,128)(2,1)}, u32[]{:S(2)}, u32[]{:S(2)}) collective-permute-start(bf16[2,256,512]{1,2,0:T(8,128)(2,1)S(1)} %get-tuple-element.306), channel_id=1, source_target_pairs={{0,28},{4,0},{8,4},{12,8},{16,12},{20,16},{24,20},{28,24},{1,29},{... | collective-permute-start | bytes 1572872 | tf_op jit(solution)/shard_map/ppermute | solution.py:12
  267.2 27.3 %copy-start.3 = (bf16[4,256,128]{1,2,0:T(8,128)(2,1)S(1)}, bf16[4,256,128]{1,2,0:T(8,128)(2,1)}, u32[]{:S(2)}) copy-start(bf16[4,256,128]{1,2,0:T(8,128)(2,1)} %get-tuple-element.71) | copy-start | bytes 786436
  301.9 5.6 %copy-start.2 = (bf16[128,2048]{1,0:T(8,128)(2,1)S(1)}, bf16[128,2048]{1,0:T(8,128)(2,1)}, u32[]{:S(2)}) copy-start(bf16[128,2048]{1,0:T(8,128)(2,1)} %param.14) | copy-start | bytes 1572868
  303.5 122.9 %copy-start.1 = (bf16[16,4096]{1,0:T(8,128)(2,1)S(1)}, bf16[16,4096]{1,0:T(8,128)(2,1)}, u32[]{:S(2)}) copy-start(bf16[16,4096]{1,0:T(8,128)(2,1)} %param.17) | copy-start | bytes 393220
  (8 other events, 11.3 us)
Sparse Core Ops, SparseCore 0:
  9.6 23.3 all-gather.2
  34.5 20.2 all-gather.4
  308.6 114.6 all-reduce.2
where the time goes:
time: 436 us; the launch traced here: 433 us
  waiting for transfers between devices  271 us (62%)
  matrix products  52.9 us (12%)
  local copies, waits for them, and re-layouts  46.3 us (11%)
  starting transfers between devices  22.4 us (5%)
  blocking collectives  14.5 us (3%)
  between operations  14.1 us (3%)
  other arithmetic  11.4 us (3%)
    ppermute x14, waiting for transfers between devices, passed_along(): lax.ppermute(value, axis, [(i, (i + by) % peers) for i in range(peers)])  113 us
    psum x1, waiting for transfers between devices, on_device(): lax.psum((down_gradient_part, up_gradient_part), ('seq', 'sub'))  112 us
    all_gather x1, waiting for transfers between devices, on_device(): total_gradient = lax.all_gather(output_gradient, 'head', axis=1, tiled=True)  24.3 us
    ppermute x14, starting transfers between devices, passed_along(): lax.ppermute(value, axis, [(i, (i + by) % peers) for i in range(peers)])  22.3 us
    all_gather x1, waiting for transfers between devices, on_device(): lax.all_gather(output_matrix, 'sub', axis=1, tiled=True)  20.2 us
    unnamed x45, local copies, waits for them, and re-layouts  19.2 us
    dot_general x8, matrix products, softmax_rows(): lax.dot_general(query_head, keys_head, (((1,), (1,)), ((), ())), preferre...  14.9 us
  transfers between devices with their start and end apart: 17, of which 10 were waited for; matrix products, arithmetic and copies ran while one was open for 8% of the time, Pallas kernels for 0%

commit v1 on v0

--- a/solution.py
+++ b/solution.py
@@ -1,6 +1,8 @@
 import jax
 import jax.numpy as jnp
 from jax import lax
+from jax.experimental import pallas as pl
+from jax.experimental.pallas import tpu as pltpu
 from jax.sharding import PartitionSpec as P
 
 HD = 128
@@ -82,7 +84,7 @@
     return (attention_output, query_gradient, pair_grads)
 
 
-def on_device(
+def on_device_windows(
     head_query_rows,
     head_key_rows,
     head_value_rows,
@@ -161,6 +163,202 @@
     )
 
 
+SCALE = HD ** (-0.5)
+F32, BF16 = jnp.float32, jnp.bfloat16
+
+
+def dot_nn(left, right):
+    return lax.dot_general(left, right, (((1,), (0,)), ((), ())), preferred_element_type=F32)
+
+
+def dot_nt(left, right):
+    return lax.dot_general(left, right, (((1,), (1,)), ((), ())), preferred_element_type=F32)
+
+
+def swapped(value, axis):
+    return lax.ppermute(value, axis, [(0, 1), (1, 0)])
+
+
+def attention_kernel(
+    blocks, place_ref, own_ref, other_ref, dout_ref, attn_ref, dq_ref, mine_ref, theirs_ref,
+    queries, keys, values, douts, keys_t, values_t, dkeys, dvalues,
+):
+    half = HD
+    sub, first = place_ref[0], place_ref[1]
+    own_at = sub * half
+    other_at = half - own_at
+
+    def gather(o, carry):
+        b = lax.rem(o + first, blocks)
+        at = pl.multiple_of(o * 2 * half, half)
+        queries[pl.ds(pl.multiple_of(o * half, half), half), :] = own_ref[b, 0]
+        douts[pl.ds(pl.multiple_of(o * half, half), half), :] = dout_ref[b]
+        keys[pl.ds(pl.multiple_of(at + own_at, half), half), :] = own_ref[b, 1]
+        values[pl.ds(pl.multiple_of(at + own_at, half), half), :] = own_ref[b, 2]
+        keys[pl.ds(pl.multiple_of(at + other_at, half), half), :] = other_ref[b, 0]
+        values[pl.ds(pl.multiple_of(at + other_at, half), half), :] = other_ref[b, 1]
+        return carry
+
+    lax.fori_loop(0, blocks, gather, 0)
+    keys_t[...] = keys[...].T
+    values_t[...] = values[...].T
+    tile = 2 * half
+    tiles = blocks // 2
+    for u in reversed(range(tiles)):
+        extent = (u + 1) * 2 * tile
+        settled = extent - 2 * tile
+        q = queries[u * tile : (u + 1) * tile, :]
+        g = douts[u * tile : (u + 1) * tile, :]
+        scores = dot_nt(keys[:extent, :], q) * SCALE
+        key_at = lax.broadcasted_iota(jnp.int32, (2 * tile, tile), 0)
+        row = lax.broadcasted_iota(jnp.int32, (2 * tile, tile), 1)
+        query_at = row + jnp.where(row >= half, half, 0) + own_at
+        edge = jnp.where(key_at <= query_at, scores[settled:, :], -jnp.inf)
+        scores = edge if settled == 0 else jnp.concatenate((scores[:settled, :], edge), axis=0)
+        powers = jnp.exp(scores - jnp.max(scores, axis=0, keepdims=True))
+        prob = powers * (1.0 / jnp.sum(powers, axis=0, keepdims=True))
+        prob_lo = prob.astype(BF16)
+        attn = dot_nn(values_t[:, :extent], prob_lo).T.astype(BF16)
+        dprob = dot_nt(values[:extent, :], g)
+        delta = jnp.sum(prob * dprob, axis=0, keepdims=True)
+        dscore = (prob * (dprob - delta) * SCALE).astype(BF16)
+        dq = dot_nn(keys_t[:, :extent], dscore).T.astype(BF16)
+        dk = dot_nn(dscore, q)
+        dv = dot_nn(prob_lo, g)
+        if u == tiles - 1:
+            dkeys[:extent, :] = dk
+            dvalues[:extent, :] = dv
+        else:
+            dkeys[:extent, :] += dk
+            dvalues[:extent, :] += dv
+        for part in range(2):
+            b = lax.rem(2 * u + part + first, blocks)
+            attn_ref[b] = attn[part * half : (part + 1) * half, :]
+            dq_ref[b] = dq[part * half : (part + 1) * half, :]
+
+    def scatter(o, carry):
+        b = lax.rem(o + first, blocks)
+        at = pl.multiple_of(o * 2 * half, half)
+        own = pl.ds(pl.multiple_of(at + own_at, half), half)
+        other = pl.ds(pl.multiple_of(at + other_at, half), half)
+        mine_ref[b, 0] = dkeys[own, :]
+        mine_ref[b, 1] = dvalues[own, :]
+        theirs_ref[b, 0] = dkeys[other, :].astype(BF16)
+        theirs_ref[b, 1] = dvalues[other, :].astype(BF16)
+        return carry
+
+    lax.fori_loop(0, blocks, scatter, 0)
+
+
+def attention(place, own, other, dout):
+    blocks = own.shape[0]
+    rows = own.shape[2]
+    total = 2 * blocks * rows
+    vmem = pl.BlockSpec(memory_space=pltpu.VMEM)
+    return pl.pallas_call(
+        lambda *refs: attention_kernel(blocks, *refs),
+        out_shape=(
+            jax.ShapeDtypeStruct((blocks, rows, HD), BF16),
+            jax.ShapeDtypeStruct((blocks, rows, HD), BF16),
+            jax.ShapeDtypeStruct((blocks, 2, rows, HD), F32),
+            jax.ShapeDtypeStruct((blocks, 2, rows, HD), BF16),
+        ),
+        in_specs=[pl.BlockSpec(memory_space=pltpu.SMEM), vmem, vmem, vmem],
+        out_specs=[vmem] * 4,
+        scratch_shapes=[
+            pltpu.VMEM((total // 2, HD), BF16),
+            pltpu.VMEM((total, HD), BF16),
+            pltpu.VMEM((total, HD), BF16),
+            pltpu.VMEM((total // 2, HD), BF16),
+            pltpu.VMEM((HD, total), BF16),
+            pltpu.VMEM((HD, total), BF16),
+            pltpu.VMEM((total, HD), F32),
+            pltpu.VMEM((total, HD), F32),
+        ],
+        compiler_params=pltpu.CompilerParams(vmem_limit_bytes=48 * 1024 * 1024),
+        cost_estimate=pl.CostEstimate(
+            flops=12 * total * total // 4 * HD, bytes_accessed=20 * total * HD, transcendentals=0
+        ),
+    )(place, own, other, dout)
+
+
+def by_head(value, heads):
+    rows = value.shape[0]
+    return value.reshape(rows, heads, HD).transpose(1, 0, 2)
+
+
+def exact(left, right):
+    return jnp.dot(left, right, preferred_element_type=F32, precision=lax.Precision.HIGHEST)
+
+
+def on_device_heads(
+    head_query_rows,
+    head_key_rows,
+    head_value_rows,
+    output_gradient,
+    output_matrix,
+    adapter_down_weight,
+    adapter_up_weight,
+):
+    rows, feats = head_query_rows.shape
+    heads = feats // HD
+    cols = output_gradient.shape[1]
+    head, sub = lax.axis_index("head"), lax.axis_index("sub")
+    gradient_away = swapped(output_gradient, "head")
+    matrix_away = swapped(output_matrix, "sub")
+    projections = jnp.stack(
+        (by_head(head_query_rows, heads), by_head(head_key_rows, heads), by_head(head_value_rows, heads)),
+        axis=1,
+    )
+    own = lax.all_to_all(projections, "seq", split_axis=0, concat_axis=0, tiled=True)
+    other = swapped(own[:, 1:], "sub")
+    same = head == sub
+    projected = dot_nt(jnp.where(same, output_gradient, gradient_away), output_matrix) + dot_nt(
+        jnp.where(same, gradient_away, output_gradient), matrix_away
+    )
+    up_here = lax.dynamic_slice_in_dim(adapter_up_weight, head * cols, cols, axis=1)
+    up_away = lax.dynamic_slice_in_dim(adapter_up_weight, (1 - head) * cols, cols, axis=1)
+    adapter_upward = dot_nt(output_gradient, up_here) + dot_nt(gradient_away, up_away)
+    adapter_backward = exact(adapter_upward, adapter_down_weight.astype(F32).T)
+    dout = (projected + 2.0 * adapter_backward).astype(BF16)
+    dout = lax.all_to_all(by_head(dout, heads), "seq", split_axis=0, concat_axis=0, tiled=True)
+    shifted = head >= lax.axis_size("head") // 2
+    place = jnp.stack((sub, jnp.where(shifted, GROUP // 2 // (2 * rows), 0))).astype(jnp.int32)
+    attn, dq, mine, theirs = attention(place, own, other, dout)
+    pair = (mine + swapped(theirs, "sub").astype(F32)).astype(BF16)
+    back = jnp.concatenate((attn[:, None], dq[:, None], pair), axis=1)
+    back = lax.all_to_all(back, "seq", split_axis=0, concat_axis=0, tiled=True)
+    attn, dq, dk, dv = [back[:, n].transpose(1, 0, 2).reshape(rows, feats) for n in range(4)]
+    middle_part = jnp.dot(attn, adapter_down_weight, preferred_element_type=F32)
+    middle = middle_part + swapped(middle_part, "head")
+    rank = middle.shape[1]
+    down_part = 2.0 * exact(adapter_upward.T, attn.astype(F32))
+    up_part = 2.0 * exact(middle.T, output_gradient.astype(F32))
+    parts = jnp.concatenate((down_part, up_part), axis=1)
+    peers = 2 * heads
+    width = parts.shape[1] // peers
+    parts = parts.reshape(rank, peers, width).transpose(1, 0, 2)
+    terms = lax.all_to_all(parts, ("seq", "sub"), split_axis=0, concat_axis=0, tiled=True)
+    piece = jnp.sum(terms, axis=0)
+    spread = jnp.broadcast_to(piece[None], (peers, rank, width))
+    whole = lax.all_to_all(spread, ("seq", "sub"), split_axis=0, concat_axis=0, tiled=True)
+    whole = whole.transpose(1, 0, 2).reshape(rank, peers * width)
+    return dq, dk, dv, whole[:, :feats].T, whole[:, feats:]
+
+
+def one_group(mesh, rows, feats, width):
+    seq, head, sub = mesh.shape["seq"], mesh.shape["head"], mesh.shape["sub"]
+    return (
+        sub == 2
+        and head == 2
+        and rows == HD
+        and seq % 2 == 0
+        and seq * sub * rows == GROUP
+        and feats == seq * HD
+        and (feats + width) % (seq * sub) == 0
+    )
+
+
 def solution(mesh):
     in_specs = (
         P(("rep", "seq", "sub"), "head"),
@@ -178,6 +376,12 @@
         P(("rep", "head"), None),
         P("rep", "head"),
     )
+
+    def on_device(*local):
+        if one_group(mesh, *local[0].shape, local[3].shape[1]):
+            return on_device_heads(*local)
+        return on_device_windows(*local)
+
     return jax.shard_map(
         on_device, mesh=mesh, in_specs=in_specs, out_specs=out_specs, check_vma=False
     )

time: 436 us -> 131 us (0.30)
  waiting for transfers between devices: 271 us -> 34.1 us
  matrix products: 52.9 us -> 7.02 us
  local copies, waits for them, and re-layouts: 46.3 us -> 11.8 us
  blocking collectives: 14.5 us -> 43.9 us
  between operations: 14.1 us -> 0.86 us
  other arithmetic: 11.4 us -> 1.34 us
  Pallas kernels: 0 us -> 9.74 us
    psum x1 -> x0, waiting for transfers between devices: 112 us -> none  [on_device(): lax.psum((down_gradient_part, up_gradient_part), ('seq', 'sub'))]
    ppermute x14 -> x5, waiting for transfers between devices: 113 us -> 14.2 us  [swapped(): return lax.ppermute(value, axis, [(0, 1), (1, 0)])]
    dot_general x34 -> x8, matrix products: 52.9 us -> 7.02 us  [the longest x4 5.81 us: dot_nt(): lax.dot_general(left, right, (((1,), (1,)), ((), ())), preferred_element_...]
    all_gather x2 -> x0, waiting for transfers between devices: 44.4 us -> none  [the longest x1 24.3 us: on_device(): total_gradient = lax.all_gather(output_gradient, 'head', axis=1, tiled=True)]
    all_to_all x2, blocking collectives: 10.5 us -> 43.9 us  [the longest x1 28 us: on_device_heads(): back = lax.all_to_all(back, 'seq', split_axis=0, concat_axis=0, tiled=True)]
    all_to_all x0 -> x3, waiting for transfers between devices: none -> 19.9 us  [the longest x1 7.42 us: on_device_heads(): lax.all_to_all(by_head(dout, heads), 'seq', split_axis=0, concat_axis=0,...]
    ppermute x14 -> x5, starting transfers between devices: 22.3 us -> 6.16 us  [swapped(): return lax.ppermute(value, axis, [(0, 1), (1, 0)])]
    all_to_all x0 -> x3, starting transfers between devices: none -> 14.5 us  [the longest x1 6.98 us: on_device_heads(): lax.all_to_all(projections, 'seq', split_axis=0, concat_axis=0, tiled=True)]
  transfers between devices with their start and end apart: 17 -> 8, of which waited for: 10 -> 6; matrix products, arithmetic and copies ran while one was open for 8% -> 13% of each run, Pallas kernels for 0% -> 0%
where the time goes in v1:
time: 131 us; the launch traced here: 129 us
  blocking collectives  43.9 us (34%)
  waiting for transfers between devices  34.1 us (26%)
  starting transfers between devices  20.7 us (16%)
  local copies, waits for them, and re-layouts  11.8 us (9%)
  Pallas kernels  9.74 us (7%)
  matrix products  7.02 us (5%)
  other arithmetic  1.34 us (1%)
    all_to_all x1, blocking collectives, on_device_heads(): back = lax.all_to_all(back, 'seq', split_axis=0, concat_axis=0, tiled=True)  28 us
    all_to_all x1, blocking collectives, on_device_heads(): lax.all_to_all(parts, ('seq', 'sub'), split_axis=0, concat_axis=0, tiled=...  15.9 us
    ppermute x5, waiting for transfers between devices, swapped(): return lax.ppermute(value, axis, [(0, 1), (1, 0)])  14.2 us
    pallas_call x1, Pallas kernels, attention(): pl.pallas_call(lambda *refs: attention_kernel(blocks, *refs), out_shape=(...  9.74 us
    all_to_all x1, waiting for transfers between devices, on_device_heads(): lax.all_to_all(by_head(dout, heads), 'seq', split_axis=0, concat_axis=0,...  7.42 us
    all_to_all x1, starting transfers between devices, on_device_heads(): lax.all_to_all(projections, 'seq', split_axis=0, concat_axis=0, tiled=True)  6.98 us
    all_to_all x1, waiting for transfers between devices, on_device_heads(): lax.all_to_all(spread, ('seq', 'sub'), split_axis=0, concat_axis=0, tiled...  6.44 us
    ppermute x5, starting transfers between devices, swapped(): return lax.ppermute(value, axis, [(0, 1), (1, 0)])  6.16 us
  transfers between devices with their start and end apart: 8, of which 6 were waited for; matrix products, arithmetic and copies ran while one was open for 13% of the time, Pallas kernels for 0%

profile of v1, /device:TPU:1, one launch (start us, length us, event | category | flops | bytes accessed | tf_op | source)
XLA Modules:
  0.0 129.4 jit_solution(14176927527827277915)
XLA Ops:
  0.8 1.2 copy.47
  2.2 1.1 copy.43
  3.5 1.1 copy.45
  4.8 1.0 pad_maximum_fusion.1
  5.8 7.0 %all-to-all-start = ((bf16[8,3,128,128]{3,2,1,0:T(8,128)(2,1)}), bf16[8,3,128,128]{3,2,1,0:T(8,128)(2,1)S(1)}, u32[]{:S(2)}, u32[]{:S(2)}) async-start(bf16[8,3,128,128]{3,2,1,0:T(8,128)(2,1)} %pad_maximum_fusion.1), calls=%async_computation | async-start | bytes 1572864 | tf_op jit(solution)/shard_map/all_to_all | solution.py:313
  12.8 1.3 collective-permute-start.1
  14.3 11.7 %collective-permute-done.1 = bf16[128,2048]{1,0:T(8,128)(2,1)S(1)} collective-permute-done((bf16[128,2048]{1,0:T(8,128)(2,1)S(1)}, bf16[128,2048]{1,0:T(8,128)(2,1)S(1)}, u32[]{:S(2)}, u32[]{:S(2)}) %collective-permute-start.1) | collective-permute-done | bytes 524320 | tf_op jit(solution)/shard_map/ppermute | solution.py:179
  26.2 0.4 convolution_multiply_fusion.1
  26.6 6.0 %all-to-all-done.refs_1_ = bf16[8,3,128,128]{3,2,1,0:T(8,128)(2,1)S(1)} async-done(((bf16[8,3,128,128]{3,2,1,0:T(8,128)(2,1)}), bf16[8,3,128,128]{3,2,1,0:T(8,128)(2,1)S(1)}, u32[]{:S(2)}, u32[]{:S(2)}) %all-to-all-start) | async-done | bytes 786464 | tf_op jit(solution)/shard_map/all_to_all | solution.py:313
  32.7 0.8 slice.28
  33.5 1.2 collective-permute-start
  34.7 3.7 %fusion.2 = f32[128,1024]{1,0:T(8,128)S(1)} fusion(bf16[1024,2048]{1,0:T(8,128)(2,1)} %collective-permute-done.2, bf16[128,2048]{1,0:T(8,128)(2,1)S(1)} %collective-permute-done.1, bf16[128,2048]{1,0:T(8,128)(2,1)S(1)} %copy-done.1, pred[]{:T(512)S(6)} %eq.3), kind=kOutput, calls=%fused_computation.10 | convolution fusion | flops 537133056 | bytes 5767169 | tf_op jit(solution)/shard_map/dot_general | solution.py:175
  38.5 1.6 %fusion.1 = bf16[128,1024]{1,0:T(8,128)(2,1)S(1)} fusion(f32[128,1024]{1,0:T(8,128)S(1)} %convolution_multiply_fusion.1, f32[128,1024]{1,0:T(8,128)S(1)} %fusion.2, bf16[1024,2048]{1,0:T(8,128)(2,1)S(1)} %copy-done.2, bf16[128,2048]{1,0:T(8,128)(2,1)S(1)} %copy-done.1, bf16[128,2048]{1,0:T(8,128)(2,1)S(1)} %collective-permute-done.1, pred[]{:T(512)S(6)} %eq.3), kind=kOutput, calls=%fused_computation.4 | convolution fusion | flops 537526272 | bytes 6553601 | tf_op jit(solution)/shard_map/dot_general | solution.py:175
  40.2 0.9 copy.50
  41.1 3.6 %all-to-all-start.1 = ((bf16[8,128,128]{2,1,0:T(8,128)(2,1)}), bf16[8,128,128]{2,1,0:T(8,128)(2,1)S(1)}, u32[]{:S(2)}, u32[]{:S(2)}) async-start(bf16[8,128,128]{2,1,0:T(8,128)(2,1)} %bitcast.12), calls=%async_computation.1 | async-start | bytes 524288 | tf_op jit(solution)/shard_map/all_to_all | solution.py:324
  44.8 7.4 %all-to-all-done.1.refs_3_ = bf16[8,128,128]{2,1,0:T(8,128)(2,1)S(1)} async-done(((bf16[8,128,128]{2,1,0:T(8,128)(2,1)}), bf16[8,128,128]{2,1,0:T(8,128)(2,1)S(1)}, u32[]{:S(2)}, u32[]{:S(2)}) %all-to-all-start.1) | async-done | bytes 262176 | tf_op jit(solution)/shard_map/all_to_all | solution.py:324
  52.2 9.7 %shard_map.110 = (bf16[8,128,128]{2,1,0:T(8,128)(2,1)S(1)}, bf16[8,128,128]{2,1,0:T(8,128)(2,1)S(1)}, f32[8,2,128,128]{3,2,1,0:T(8,128)S(1)}, bf16[8,2,128,128]{3,2,1,0:T(8,128)(2,1)S(1)}) custom-call(s32[2]{0:T(128)S(1)} %pad_add_fusion.refs_0_, bf16[8,3,128,128]{3,2,1,0:T(8,128)(2,1)S(1)} %all-to-all-done.refs_1_, ...), custom_call_target="tpu_custom_call" | custom-call | flops 1610612736 | bytes 5242880 | tf_op jit(solution)/shard_map/pallas_call | solution.py:258
  61.9 2.3 %collective-permute-start.3 = (bf16[8,2,128,128]{3,2,1,0:T(8,128)(2,1)S(1)}, bf16[8,2,128,128]{3,2,1,0:T(8,128)(2,1)S(1)}, u32[]{:S(2)}, u32[]{:S(2)}) collective-permute-start(bf16[8,2,128,128]{3,2,1,0:T(8,128)(2,1)S(1)} %get-tuple-element.12), channel_id=1, source_target_pairs={{0,1},{1,0},{2,3},{3,2},{4,5},{5,4},{6,7},{7,6},{8,9},{9,8},{10,11... | collective-permute-start | bytes 1572872 | tf_op jit(solution)/shard_map/ppermute | solution.py:179
  64.3 1.5 %collective-permute-done.3 = bf16[8,2,128,128]{3,2,1,0:T(8,128)(2,1)S(1)} collective-permute-done((bf16[8,2,128,128]{3,2,1,0:T(8,128)(2,1)S(1)}, bf16[8,2,128,128]{3,2,1,0:T(8,128)(2,1)S(1)}, u32[]{:S(2)}, u32[]{:S(2)}) %collective-permute-start.3) | collective-permute-done | bytes 524320 | tf_op jit(solution)/shard_map/ppermute | solution.py:179
  66.1 28.0 %all_to_all.25 = bf16[8,4,128,128]{3,2,1,0:T(8,128)(2,1)S(1)} all-to-all(bf16[8,4,128,128]{3,2,1,0:T(8,128)(2,1)S(1)} %pad_maximum_fusion), channel_id=1, replica_groups=mesh['rep'=1,'seq'=8,'head'=2,'sub'=2] {'seq'}, dimensions={0} | all-to-all | bytes 2097152 | tf_op jit(solution)/shard_map/all_to_all | solution.py:330
  94.5 1.2 collective-permute-start.4
  96.0 1.0 collective-permute-done.4
  97.0 0.3 convolution_multiply_fusion
  97.6 15.9 %all_to_all.26 = f32[16,16,192]{2,1,0:T(8,128)S(1)} all-to-all(f32[16,16,192]{2,1,0:T(8,128)S(1)} %bitcast.61), channel_id=1, replica_groups=mesh['rep'=1,'seq'=8,'head'=2,'sub'=2] {'seq','sub'}, dimensions={0} | all-to-all | bytes 393216 | tf_op jit(solution)/shard_map/all_to_all | solution.py:341
  113.6 0.7 broadcast_in_dim.14
  114.3 4.0 %all-to-all-start.4 = ((f32[16,16,192]{2,1,0:T(8,128)}), f32[16,16,192]{2,1,0:T(8,128)S(1)}, u32[]{:S(2)}, u32[]{:S(2)}) async-start(f32[16,16,192]{2,1,0:T(8,128)} %broadcast_in_dim.14), calls=%async_computation.4 | async-start | bytes 524288 | tf_op jit(solution)/shard_map/all_to_all | solution.py:344
  118.5 0.9 copy.57
  119.5 0.9 copy.58
  120.5 0.9 copy.59
  121.4 6.4 %all-to-all-done.4 = f32[16,16,192]{2,1,0:T(8,128)S(1)} async-done(((f32[16,16,192]{2,1,0:T(8,128)}), f32[16,16,192]{2,1,0:T(8,128)S(1)}, u32[]{:S(2)}, u32[]{:S(2)}) %all-to-all-start.4) | async-done | bytes 196640 | tf_op jit(solution)/shard_map/all_to_all | solution.py:344
  128.1 0.7 slice.34
  128.8 0.6 slice_bitcast_fusion.4
  (35 shorter events, 3.5 us)
Async XLA Ops:
  0.6 13.4 %copy-start = (bf16[16,4096]{1,0:T(8,128)(2,1)S(1)}, bf16[16,4096]{1,0:T(8,128)(2,1)}, u32[]{:S(2)}) copy-start(bf16[16,4096]{1,0:T(8,128)(2,1)} %param.13) | copy-start | bytes 393220
  0.6 12.1 %copy-start.1 = (bf16[128,2048]{1,0:T(8,128)(2,1)S(1)}, bf16[128,2048]{1,0:T(8,128)(2,1)}, u32[]{:S(2)}) copy-start(bf16[128,2048]{1,0:T(8,128)(2,1)} %param.10) | copy-start | bytes 1572868
  0.7 25.5 %copy-start.3 = (bf16[1024,16]{0,1:T(8,128)(2,1)S(1)}, bf16[1024,16]{0,1:T(8,128)(2,1)}, u32[]{:S(2)}) copy-start(bf16[1024,16]{0,1:T(8,128)(2,1)} %param.12) | copy-start | bytes 98308
  0.7 34.0 %collective-permute-start.2 = (bf16[1024,2048]{1,0:T(8,128)(2,1)}, bf16[1024,2048]{1,0:T(8,128)(2,1)}, u32[]{:S(2)}, u32[]{:S(2)}) collective-permute-start(bf16[1024,2048]{1,0:T(8,128)(2,1)} %param.11), channel_id=1, source_target_pairs={{0,1},{1,0},{2,3},{3,2},{4,5},{5,4},{6,7},{7,6},{8,9},{9,8},{10,11... | collective-permute-start | bytes 12582920 | tf_op jit(solution)/shard_map/ppermute | solution.py:179
  5.8 26.9 %all-to-all-start = ((bf16[8,3,128,128]{3,2,1,0:T(8,128)(2,1)}), bf16[8,3,128,128]{3,2,1,0:T(8,128)(2,1)S(1)}, u32[]{:S(2)}, u32[]{:S(2)}) async-start(bf16[8,3,128,128]{3,2,1,0:T(8,128)(2,1)} %pad_maximum_fusion.1), calls=%async_computation | async-start | bytes 1572864 | tf_op jit(solution)/shard_map/all_to_all | solution.py:313
  12.8 13.2 %collective-permute-start.1 = (bf16[128,2048]{1,0:T(8,128)(2,1)S(1)}, bf16[128,2048]{1,0:T(8,128)(2,1)S(1)}, u32[]{:S(2)}, u32[]{:S(2)}) collective-permute-start(bf16[128,2048]{1,0:T(8,128)(2,1)S(1)} %copy-done.1), channel_id=1, source_target_pairs={{0,2},{2,0},{1,3},{3,1},{4,6},{6,4},{5,7},{7,5},{8,10},{10,8},{9,1... | collective-permute-start | bytes 1572872 | tf_op jit(solution)/shard_map/ppermute | solution.py:179
  32.7 5.8 %copy-start.2 = (bf16[1024,2048]{1,0:T(8,128)(2,1)S(1)}, bf16[1024,2048]{1,0:T(8,128)(2,1)}, u32[]{:S(2)}) copy-start(bf16[1024,2048]{1,0:T(8,128)(2,1)} %param.11) | copy-start | bytes 12582916
  33.5 11.3 %collective-permute-start = (bf16[8,2,128,128]{3,2,1,0:T(8,128)(2,1)}, bf16[8,2,128,128]{3,2,1,0:T(8,128)(2,1)S(1)}, u32[]{:S(2)}, u32[]{:S(2)}) collective-permute-start(bf16[8,2,128,128]{3,2,1,0:T(8,128)(2,1)} %slice.28), channel_id=1, source_target_pairs={{0,1},{1,0},{2,3},{3,2},{4,5},{5,4},{6,7},{7,6},{8,9},{9,8},{10,11... | collective-permute-start | bytes 1572872 | tf_op jit(solution)/shard_map/ppermute | solution.py:179
  41.1 11.1 %all-to-all-start.1 = ((bf16[8,128,128]{2,1,0:T(8,128)(2,1)}), bf16[8,128,128]{2,1,0:T(8,128)(2,1)S(1)}, u32[]{:S(2)}, u32[]{:S(2)}) async-start(bf16[8,128,128]{2,1,0:T(8,128)(2,1)} %bitcast.12), calls=%async_computation.1 | async-start | bytes 524288 | tf_op jit(solution)/shard_map/all_to_all | solution.py:324
  61.9 3.9 %collective-permute-start.3 = (bf16[8,2,128,128]{3,2,1,0:T(8,128)(2,1)S(1)}, bf16[8,2,128,128]{3,2,1,0:T(8,128)(2,1)S(1)}, u32[]{:S(2)}, u32[]{:S(2)}) collective-permute-start(bf16[8,2,128,128]{3,2,1,0:T(8,128)(2,1)S(1)} %get-tuple-element.12), channel_id=1, source_target_pairs={{0,1},{1,0},{2,3},{3,2},{4,5},{5,4},{6,7},{7,6},{8,9},{9,8},{10,11... | collective-permute-start | bytes 1572872 | tf_op jit(solution)/shard_map/ppermute | solution.py:179
  65.8 28.5 %copy-start.4 = (bf16[1024,16]{0,1:T(8,128)(2,1)S(1)}, bf16[1024,16]{0,1:T(8,128)(2,1)}, u32[]{:S(2)}) copy-start(bf16[1024,16]{0,1:T(8,128)(2,1)} %param.12) | copy-start | bytes 98308
  94.5 2.5 %collective-permute-start.4 = (f32[128,16]{0,1:T(8,128)S(1)}, f32[128,16]{0,1:T(8,128)S(1)}, u32[]{:S(2)}, u32[]{:S(2)}) collective-permute-start(f32[128,16]{0,1:T(8,128)S(1)} %fusion.13), channel_id=1, source_target_pairs={{0,2},{2,0},{1,3},{3,1},{4,6},{6,4},{5,7},{7,5},{8,10},{10,8},{9,1... | collective-permute-start | bytes 24584 | tf_op jit(solution)/shard_map/ppermute | solution.py:179
  114.3 13.5 %all-to-all-start.4 = ((f32[16,16,192]{2,1,0:T(8,128)}), f32[16,16,192]{2,1,0:T(8,128)S(1)}, u32[]{:S(2)}, u32[]{:S(2)}) async-start(f32[16,16,192]{2,1,0:T(8,128)} %broadcast_in_dim.14), calls=%async_computation.4 | async-start | bytes 524288 | tf_op jit(solution)/shard_map/all_to_all | solution.py:344

commit v2 on v0

--- a/solution.py
+++ b/solution.py
@@ -1,6 +1,8 @@
 import jax
 import jax.numpy as jnp
 from jax import lax
+from jax.experimental import pallas as pl
+from jax.experimental.pallas import tpu as pltpu
 from jax.sharding import PartitionSpec as P
 
 HD = 128
@@ -82,7 +84,7 @@
     return (attention_output, query_gradient, pair_grads)
 
 
-def on_device(
+def on_device_windows(
     head_query_rows,
     head_key_rows,
     head_value_rows,
@@ -161,6 +163,481 @@
     )
 
 
+SCALE = HD ** (-0.5)
+F32, BF16 = jnp.float32, jnp.bfloat16
+LOOK, DQ, DK, DV = range(4)
+
+
+def dot_nn(left, right):
+    return lax.dot_general(left, right, (((1,), (0,)), ((), ())), preferred_element_type=F32)
+
+
+def dot_nt(left, right):
+    return lax.dot_general(left, right, (((1,), (1,)), ((), ())), preferred_element_type=F32)
+
+
+def dot_tn(left, right):
+    return lax.dot_general(left, right, (((0,), (0,)), ((), ())), preferred_element_type=F32)
+
+
+def three_terms(value):
+    high = value.astype(BF16)
+    rest = value - high.astype(F32)
+    mid = rest.astype(BF16)
+    low = (rest - mid.astype(F32)).astype(BF16)
+    return jnp.concatenate((high, mid, low), axis=0)
+
+
+def folded(product):
+    rank = product.shape[0] // 3
+    return product[:rank] + product[rank : 2 * rank] + product[2 * rank :]
+
+
+def whole_kernel(
+    n_seq,
+    q_ref, k_ref, v_ref, g_ref, w_ref, down_ref, up_ref,
+    dq_ref, dk_ref, dv_ref, down_out, up_out,
+    g_all, w_all, queries, keys, values, douts, dout_send,
+    keys_t, values_t, probs, attn_send, dq_send, attn_full, dkeys, dvalues,
+    pair_send, pair_recv, pair_sum, upward, mid_mine, mid_theirs, pieces, gathered, totals,
+    local_sem, swap_send, swap_recv, in_send, in_recv, in_local, kv_send, kv_recv,
+    do_send, do_recv, back_send, back_recv, back_local, pair_ssem, pair_rsem,
+    rs_send, rs_recv, ag_send, ag_recv,
+):
+    me, head, sub = lax.axis_index("seq"), lax.axis_index("head"), lax.axis_index("sub")
+    rank = down_ref.shape[0]
+    feats = down_ref.shape[1]
+    cols = g_ref.shape[1]
+    peers = 2 * n_seq
+    mine = me * 2 + sub
+    first = head * (n_seq // 2)
+    own_at = sub * HD
+
+    def ring(n):
+        return lax.rem(me + n, n_seq)
+
+    def place_of(block):
+        return lax.rem(block - first + n_seq, n_seq)
+
+    def rows_of(order, which):
+        return pl.ds(pl.multiple_of(order * (2 * HD) + which * HD, HD), HD)
+
+    def own_rows(order):
+        return pl.ds(pl.multiple_of(order * HD, HD), HD)
+
+    def lanes(block):
+        return pl.ds(pl.multiple_of(block * HD, HD), HD)
+
+    def remote(src, dst, send, recv, device):
+        return pltpu.make_async_remote_copy(
+            src_ref=src, dst_ref=dst, send_sem=send, recv_sem=recv,
+            device_id=device, device_id_type=pl.DeviceIdType.MESH,
+        )
+
+    def across(src, dst, send, recv, device):
+        return remote(src, dst, send, recv, {"seq": device})
+
+    barrier = pltpu.get_barrier_semaphore()
+
+    def greet(n, carry):
+        p = lax.rem(mine + n, peers)
+        pl.semaphore_signal(
+            barrier, inc=1, device_id={"seq": p // 2, "sub": lax.rem(p, 2)},
+            device_id_type=pl.DeviceIdType.MESH,
+        )
+        return carry
+
+    own_g = pltpu.make_async_copy(g_ref, g_all.at[head], local_sem.at[0])
+    own_w = pltpu.make_async_copy(w_ref, w_all.at[sub], local_sem.at[1])
+    own_g.start()
+    own_w.start()
+    lax.fori_loop(1, peers, greet, 0)
+    pl.semaphore_signal(
+        barrier, inc=1, device_id={"head": 1 - head}, device_id_type=pl.DeviceIdType.MESH
+    )
+    pl.semaphore_wait(barrier, peers)
+
+    g_swap = remote(g_ref, g_all.at[head], swap_send.at[0], swap_recv.at[0], {"head": 1 - head})
+    w_swap = remote(w_ref, w_all.at[sub], swap_send.at[1], swap_recv.at[1], {"sub": 1 - sub})
+    g_swap.start()
+    w_swap.start()
+
+    o_me = place_of(me)
+
+    def inward(n, carry):
+        to = ring(n)
+        for t, (src, dst, at) in enumerate(
+            (
+                (k_ref, keys, rows_of(o_me, sub)),
+                (v_ref, values, rows_of(o_me, sub)),
+                (q_ref, queries, own_rows(o_me)),
+            )
+        ):
+            across(
+                src.at[:, lanes(to)], dst.at[at, :], in_send.at[t, to], in_recv.at[t, me], to
+            ).start()
+        return carry
+
+    lax.fori_loop(1, n_seq, inward, 0)
+    own_in = [
+        pltpu.make_async_copy(src.at[:, lanes(me)], dst.at[at, :], in_local.at[t])
+        for t, (src, dst, at) in enumerate(
+            (
+                (k_ref, keys, rows_of(o_me, sub)),
+                (v_ref, values, rows_of(o_me, sub)),
+                (q_ref, queries, own_rows(o_me)),
+            )
+        )
+    ]
+    for copy in own_in:
+        copy.start()
+
+    own_g.wait()
+    own_w.wait()
+    g_swap.wait()
+    upward[...] = dot_nt(up_ref[:, :cols], g_all[0]) + dot_nt(up_ref[:, cols:], g_all[1])
+    w_swap.wait()
+    up_terms = three_terms(upward[...])
+
+    def dout_of(h):
+        rows = pl.ds(pl.multiple_of(h * HD, HD), HD)
+        projected = dot_nt(g_all[0], w_all[0, rows, :]) + dot_nt(g_all[1], w_all[1, rows, :])
+        down = down_ref[:, lanes(h)]
+        adapter = dot_tn(up_terms, jnp.concatenate((down, down, down), axis=0))
+        return (projected + 2.0 * adapter).astype(BF16)
+
+    def send_dout(n, carry):
+        to = ring(n)
+        dout_send[to] = dout_of(to)
+        across(
+            dout_send.at[to], douts.at[own_rows(o_me), :], do_send.at[to], do_recv.at[me], to
+        ).start()
+        return carry
+
+    lax.fori_loop(1, n_seq, send_dout, 0)
+    douts[own_rows(o_me), :] = dout_of(me)
+
+    for copy in own_in:
+        copy.wait()
+
+    def kv_copy(t, order):
+        dst = keys if t == 0 else values
+        at = rows_of(order, sub)
+        return remote(
+            dst.at[at, :], dst.at[at, :], kv_send.at[t, order], kv_recv.at[t, order],
+            {"sub": 1 - sub},
+        )
+
+    def in_wait(t, frm):
+        dst, at = (
+            (keys, rows_of(place_of(frm), sub)),
+            (values, rows_of(place_of(frm), sub)),
+            (queries, own_rows(place_of(frm))),
+        )[t]
+        src = (k_ref, v_ref, q_ref)[t]
+        return across(src.at[:, lanes(frm)], dst.at[at, :], in_send.at[t, frm], in_recv.at[t, frm], frm)
+
+    kv_copy(0, o_me).start()
+    kv_copy(1, o_me).start()
+
+    def hand_on(n, carry):
+        frm = ring(n_seq - n)
+        for t in range(2):
+            in_wait(t, frm).wait_recv()
+            kv_copy(t, place_of(frm)).start()
+        in_wait(2, frm).wait_recv()
+        return carry
+
+    lax.fori_loop(1, n_seq, hand_on, 0)
+
+    def kv_arrived(order, carry):
+        for t in range(2):
+            dst = keys if t == 0 else values
+            at = rows_of(order, 1 - sub)
+            remote(
+                dst.at[at, :], dst.at[at, :], kv_send.at[t, order], kv_recv.at[t, order],
+                {"sub": 1 - sub},
+            ).wait_recv()
+            kv_copy(t, order).wait_send()
+        return carry
+
+    lax.fori_loop(0, n_seq, kv_arrived, 0)
+    keys_t[...] = keys[...].T
+    values_t[...] = values[...].T
+
+    sinks = (attn_full, dq_ref, dk_ref, dv_ref)
+
+    def give(kind, src, order):
+        to = lax.rem(order + first, n_seq)
+        dst = sinks[kind].at[:, lanes(me)]
+
+        @pl.when(to == me)
+        def _():
+            pltpu.make_async_copy(src, dst, back_local.at[kind]).start()
+
+        @pl.when(to != me)
+        def _():
+            across(src, dst, back_send.at[kind, to], back_recv.at[kind, me], to).start()
+
+    def settle(kind):
+        src = attn_send.at[own_rows(0), :]
+        pltpu.make_async_copy(src, sinks[kind].at[:, lanes(me)], back_local.at[kind]).wait()
+
+        def one(n, carry):
+            peer = ring(n)
+            copy = across(
+                src, sinks[kind].at[:, lanes(peer)], back_send.at[kind, peer],
+                back_recv.at[kind, peer], peer,
+            )
+            copy.wait_send()
+            copy.wait_recv()
+            return carry
+
+        lax.fori_loop(1, n_seq, one, 0)
+
+    tile = 2 * HD
+    tiles = n_seq // 2
+
+    def span(u):
+        return u * (u + 1) * tile, (u + 1) * 2 * tile
+
+    for u in reversed(range(tiles)):
+        base, extent = span(u)
+        settled = extent - 2 * tile
+        q = queries[u * tile : (u + 1) * tile, :]
+        scores = dot_nt(keys[:extent, :], q) * SCALE
+        key_at = lax.broadcasted_iota(jnp.int32, (2 * tile, tile), 0)
+        row = lax.broadcasted_iota(jnp.int32, (2 * tile, tile), 1)
+        query_at = row + jnp.where(row >= HD, HD, 0) + own_at
+        edge = jnp.where(key_at <= query_at, scores[settled:, :], -jnp.inf)
+        scores = edge if settled == 0 else jnp.concatenate((scores[:settled, :], edge), axis=0)
+        powers = jnp.exp(scores - jnp.max(scores, axis=0, keepdims=True))
+        prob = powers * (1.0 / jnp.sum(powers, axis=0, keepdims=True))
+        probs[base : base + extent, :] = prob
+        attn = dot_nn(values_t[:, :extent], prob.astype(BF16)).T.astype(BF16)
+        attn_send[u * tile : (u + 1) * tile, :] = attn
+        for order in (2 * u, 2 * u + 1):
+            give(LOOK, attn_send.at[order * HD : (order + 1) * HD, :], order)
+
+    def dout_arrived(n, carry):
+        frm = ring(n)
+        copy = across(
+            dout_send.at[frm], douts.at[own_rows(place_of(frm)), :], do_send.at[frm],
+            do_recv.at[frm], frm,
+        )
+        copy.wait_send()
+        copy.wait_recv()
+        return carry
+
+    lax.fori_loop(1, n_seq, dout_arrived, 0)
+
+    def pair_copy(u):
+        return remote(
+            pair_send.at[u], pair_recv.at[u], pair_ssem.at[u], pair_rsem.at[u], {"sub": 1 - sub}
+        )
+
+    def pair_out(u):
+        pair_copy(u).wait()
+        for part in range(2):
+            order = 2 * u + part
+            at = rows_of(order, sub)
+            for t, total in enumerate((dkeys, dvalues)):
+                pair_sum[u, t, part] = (total[at, :] + pair_recv[u, t, part].astype(F32)).astype(BF16)
+                give(DK + t, pair_sum.at[u, t, part], order)
+
+    mid_copy = remote(mid_mine, mid_theirs, swap_send.at[2], swap_recv.at[2], {"head": 1 - head})
+
+    def lora_middle():
+        settle(LOOK)
+        mid_mine[...] = dot_nt(down_ref[...], attn_full[...])
+        mid_copy.start()
+
+    def peer_id(p):
+        return {"seq": p // 2, "sub": lax.rem(p, 2)}
+
+    def lora_parts():
+        mid_copy.wait()
+        middle = mid_mine[...] + mid_theirs[...]
+        up_part = 2.0 * folded(dot_nn(three_terms(middle), g_all[head]))
+        down_part = 2.0 * folded(dot_nn(three_terms(upward[...]), attn_full[...]))
+        stack = jnp.concatenate((down_part, up_part[:, :feats], up_part[:, feats:]), axis=0)
+        half = stack.shape[0] // 2
+        for c in range(n_seq):
+            pieces[c] = stack[:half, c * HD : (c + 1) * HD]
+            pieces[n_seq + c] = stack[half:, c * HD : (c + 1) * HD]
+        gathered[mine] = pieces[mine]
+
+        def one(n, carry):
+            p = lax.rem(mine + n, peers)
+            remote(
+                pieces.at[p], gathered.at[mine], rs_send.at[p], rs_recv.at[mine], peer_id(p)
+            ).start()
+            return carry
+
+        lax.fori_loop(1, peers, one, 0)
+
+    def lora_total():
+        def one(n, carry):
+            p = lax.rem(mine + n, peers)
+            copy = remote(pieces.at[p], gathered.at[p], rs_send.at[p], rs_recv.at[p], peer_id(p))
+            copy.wait_send()
+            copy.wait_recv()
+            return carry
+
+        lax.fori_loop(1, peers, one, 0)
+        totals[mine] = jnp.sum(gathered[...], axis=0)
+
+        def share(n, carry):
+            p = lax.rem(mine + n, peers)
+            remote(
+                totals.at[mine], totals.at[mine], ag_send.at[p], ag_recv.at[mine], peer_id(p)
+            ).start()
+            return carry
+
+        lax.fori_loop(1, peers, share, 0)
+
+    def lora_end():
+        def one(n, carry):
+            p = lax.rem(mine + n, peers)
+            remote(totals.at[mine], totals.at[mine], ag_send.at[p], ag_recv.at[mine], peer_id(p)).wait_send()
+            remote(totals.at[p], totals.at[p], ag_send.at[p], ag_recv.at[p], peer_id(p)).wait_recv()
+            return carry
+
+        lax.fori_loop(1, peers, one, 0)
+        over = rank // 2
+        for c in range(n_seq):
+            at = slice(c * HD, (c + 1) * HD)
+            down_out[:, at] = totals[c, :rank, :]
+            up_out[:over, at] = totals[c, rank:, :]
+            up_out[over:, at] = totals[n_seq + c, :over, :]
+            up_out[:, feats + c * HD : feats + (c + 1) * HD] = totals[n_seq + c, over:, :]
+
+    for u in reversed(range(tiles)):
+        base, extent = span(u)
+        q = queries[u * tile : (u + 1) * tile, :]
+        g = douts[u * tile : (u + 1) * tile, :]
+        prob = probs[base : base + extent, :]
+        dprob = dot_nt(values[:extent, :], g)
+        delta = jnp.sum(prob * dprob, axis=0, keepdims=True)
+        dscore = (prob * (dprob - delta) * SCALE).astype(BF16)
+        dq_send[u * tile : (u + 1) * tile, :] = dot_nn(keys_t[:, :extent], dscore).T.astype(BF16)
+        for order in (2 * u, 2 * u + 1):
+            give(DQ, dq_send.at[order * HD : (order + 1) * HD, :], order)
+        dk = dot_nn(dscore, q)
+        dv = dot_nn(prob.astype(BF16), g)
+        if u == tiles - 1:
+            dkeys[:extent, :] = dk
+            dvalues[:extent, :] = dv
+        else:
+            dkeys[:extent, :] += dk
+            dvalues[:extent, :] += dv
+        for part in range(2):
+            at = rows_of(2 * u + part, 1 - sub)
+            pair_send[u, 0, part] = dkeys[at, :].astype(BF16)
+            pair_send[u, 1, part] = dvalues[at, :].astype(BF16)
+        pair_copy(u).start()
+        if u < tiles - 1:
+            pair_out(u + 1)
+        if u == tiles - 1:
+            lora_middle()
+        if u == tiles - 2:
+            lora_parts()
+    pair_out(0)
+    lora_total()
+
+    def in_sent(n, carry):
+        for t in range(3):
+            in_wait(t, ring(n)).wait_send()
+        return carry
+
+    lax.fori_loop(1, n_seq, in_sent, 0)
+    lora_end()
+    for kind in (DQ, DK, DV):
+        settle(kind)
+
+
+def on_device_heads(
+    head_query_rows,
+    head_key_rows,
+    head_value_rows,
+    output_gradient,
+    output_matrix,
+    adapter_down_weight,
+    adapter_up_weight,
+):
+    rows, feats = head_query_rows.shape
+    n_seq = feats // HD
+    cols = output_gradient.shape[1]
+    rank = adapter_up_weight.shape[0]
+    total = 2 * n_seq * rows
+    tiles = n_seq // 2
+    pieces = 3 * rank * feats // (2 * n_seq * HD)
+    vmem = pl.BlockSpec(memory_space=pltpu.VMEM)
+    anywhere = pl.BlockSpec(memory_space=pl.ANY)
+    dma = pltpu.SemaphoreType.DMA
+    dq, dk, dv, down, up = pl.pallas_call(
+        lambda *refs: whole_kernel(n_seq, *refs),
+        out_shape=[jax.ShapeDtypeStruct((rows, feats), BF16)] * 3
+        + [jax.ShapeDtypeStruct((rank, feats), F32), jax.ShapeDtypeStruct((rank, cols), F32)],
+        in_specs=[anywhere] * 5 + [vmem] * 2,
+        out_specs=[anywhere] * 3 + [vmem] * 2,
+        scratch_shapes=[
+            pltpu.VMEM((2, rows, cols), BF16),
+            pltpu.VMEM((2, feats, cols), BF16),
+            pltpu.VMEM((total // 2, HD), BF16),
+            pltpu.VMEM((total, HD), BF16),
+            pltpu.VMEM((total, HD), BF16),
+            pltpu.VMEM((total // 2, HD), BF16),
+            pltpu.VMEM((n_seq, rows, HD), BF16),
+            pltpu.VMEM((HD, total), BF16),
+            pltpu.VMEM((HD, total), BF16),
+            pltpu.VMEM((tiles * (tiles + 1) * 2 * HD, 2 * HD), F32),
+            pltpu.VMEM((total // 2, HD), BF16),
+            pltpu.VMEM((total // 2, HD), BF16),
+            pltpu.VMEM((rows, feats), BF16),
+            pltpu.VMEM((total, HD), F32),
+            pltpu.VMEM((total, HD), F32),
+            pltpu.VMEM((tiles, 2, 2, rows, HD), BF16),
+            pltpu.VMEM((tiles, 2, 2, rows, HD), BF16),
+            pltpu.VMEM((tiles, 2, 2, rows, HD), BF16),
+            pltpu.VMEM((rank, rows), F32),
+            pltpu.VMEM((rank, rows), F32),
+            pltpu.VMEM((rank, rows), F32),
+            pltpu.VMEM((2 * n_seq, pieces, HD), F32),
+            pltpu.VMEM((2 * n_seq, pieces, HD), F32),
+            pltpu.VMEM((2 * n_seq, pieces, HD), F32),
+            dma((2,)), dma((3,)), dma((3,)),
+            dma((3, n_seq)), dma((3, n_seq)), dma((3,)),
+            dma((2, n_seq)), dma((2, n_seq)),
+            dma((n_seq,)), dma((n_seq,)),
+            dma((4, n_seq)), dma((4, n_seq)), dma((4,)),
+            dma((tiles,)), dma((tiles,)),
+            dma((2 * n_seq,)), dma((2 * n_seq,)), dma((2 * n_seq,)), dma((2 * n_seq,)),
+        ],
+        compiler_params=pltpu.CompilerParams(
+            collective_id=0, has_side_effects=True, vmem_limit_bytes=48 * 1024 * 1024
+        ),
+    )(
+        head_query_rows, head_key_rows, head_value_rows, output_gradient, output_matrix,
+        adapter_down_weight.T, adapter_up_weight,
+    )
+    return dq, dk, dv, down.T, up
+
+
+def one_group(mesh, rows, feats, width, lora):
+    seq, head, sub = mesh.shape["seq"], mesh.shape["head"], mesh.shape["sub"]
+    return (
+        sub == 2
+        and head == 2
+        and rows == HD
+        and seq % 2 == 0
+        and seq * sub * rows == GROUP
+        and feats == seq * HD
+        and width == 2 * feats
+        and lora == 16
+    )
+
+
 def solution(mesh):
     in_specs = (
         P(("rep", "seq", "sub"), "head"),
@@ -178,6 +655,11 @@
         P(("rep", "head"), None),
         P("rep", "head"),
     )
+    def on_device(*local):
+        if one_group(mesh, *local[0].shape, local[3].shape[1], local[6].shape[0]):
+            return on_device_heads(*local)
+        return on_device_windows(*local)
+
     return jax.shard_map(
         on_device, mesh=mesh, in_specs=in_specs, out_specs=out_specs, check_vma=False
     )

time: 436 us -> 80.4 us (0.18)
  waiting for transfers between devices: 271 us -> 0 us
  Pallas kernels: 0 us -> 70.1 us
  matrix products: 52.9 us -> 0 us
  local copies, waits for them, and re-layouts: 46.3 us -> 8.94 us
  starting transfers between devices: 22.4 us -> 0 us
  blocking collectives: 14.5 us -> 0 us
  between operations: 14.1 us -> 0.66 us
  other arithmetic: 11.4 us -> 0 us
    ppermute x14 -> x0, waiting for transfers between devices: 113 us -> none  [passed_along(): lax.ppermute(value, axis, [(i, (i + by) % peers) for i in range(peers)])]
    psum x1 -> x0, waiting for transfers between devices: 112 us -> none  [on_device(): lax.psum((down_gradient_part, up_gradient_part), ('seq', 'sub'))]
    pallas_call x0 -> x1, Pallas kernels: none -> 70.1 us  [on_device_heads(): pl.pallas_call(lambda *refs: whole_kernel(n_seq, *refs), out_shape=[jax.S...]
    dot_general x34 -> x0, matrix products: 52.9 us -> none  [the longest x8 14.9 us: softmax_rows(): lax.dot_general(query_head, keys_head, (((1,), (1,)), ((), ())), preferre...]
    all_gather x2 -> x0, waiting for transfers between devices: 44.4 us -> none  [the longest x1 24.3 us: on_device(): total_gradient = lax.all_gather(output_gradient, 'head', axis=1, tiled=True)]
    ppermute x14 -> x0, starting transfers between devices: 22.3 us -> none  [passed_along(): lax.ppermute(value, axis, [(i, (i + by) % peers) for i in range(peers)])]
    all_to_all x2 -> x0, blocking collectives: 10.5 us -> none  [the longest x1 6.02 us: on_device(): lax.all_to_all(back, 'sub', split_axis=1, concat_axis=2, tiled=True)]
    unnamed x45 -> x17, local copies, waits for them, and re-layouts: 19.2 us -> 8.94 us
  transfers between devices with their start and end apart: 17 -> 0, of which waited for: 10 -> 0; matrix products, arithmetic and copies ran while one was open for 8% -> 0% of each run, Pallas kernels for 0% -> 0%
where the time goes in v2:
time: 80.4 us; the launch traced here: 79.7 us
  Pallas kernels  70.1 us (87%)
  local copies, waits for them, and re-layouts  8.94 us (11%)
    pallas_call x1, Pallas kernels, on_device_heads(): pl.pallas_call(lambda *refs: whole_kernel(n_seq, *refs), out_shape=[jax.S...  70.1 us
    unnamed x17, local copies, waits for them, and re-layouts  8.94 us

profile of v2, /device:TPU:1, one launch (start us, length us, event | category | flops | bytes accessed | tf_op | source)
XLA Modules:
  0.0 79.7 jit_solution(18143718151993526801)
XLA Ops:
  0.6 0.0 copy-start
  0.6 1.0 %copy-done = bf16[128,2048]{1,0:T(8,128)(2,1)S(1)} copy-done((bf16[128,2048]{1,0:T(8,128)(2,1)S(1)}, bf16[128,2048]{1,0:T(8,128)(2,1)}, u32[]{:S(2)}) %copy-start) | copy-done | bytes 524312
  1.7 0.0 copy-start.1
  1.7 0.9 %copy-done.1 = bf16[128,1024]{1,0:T(8,128)(2,1)S(1)} copy-done((bf16[128,1024]{1,0:T(8,128)(2,1)S(1)}, bf16[128,1024]{1,0:T(8,128)(2,1)}, u32[]{:S(2)}) %copy-start.1) | copy-done | bytes 262168
  2.6 0.0 copy-start.2
  2.6 0.9 %copy-done.2 = bf16[128,1024]{1,0:T(8,128)(2,1)S(1)} copy-done((bf16[128,1024]{1,0:T(8,128)(2,1)S(1)}, bf16[128,1024]{1,0:T(8,128)(2,1)}, u32[]{:S(2)}) %copy-start.2) | copy-done | bytes 262168
  3.6 0.0 copy-start.3
  3.6 0.9 %copy-done.3 = bf16[128,1024]{1,0:T(8,128)(2,1)S(1)} copy-done((bf16[128,1024]{1,0:T(8,128)(2,1)S(1)}, bf16[128,1024]{1,0:T(8,128)(2,1)}, u32[]{:S(2)}) %copy-start.3) | copy-done | bytes 262168
  4.5 0.0 copy-start.4
  4.5 0.9 %copy-done.4 = bf16[16,4096]{1,0:T(8,128)(2,1)S(1)} copy-done((bf16[16,4096]{1,0:T(8,128)(2,1)S(1)}, bf16[16,4096]{1,0:T(8,128)(2,1)}, u32[]{:S(2)}) %copy-start.4) | copy-done | bytes 131096
  5.4 0.0 copy-start.5
  5.4 0.8 copy-done.5
  6.2 70.1 %shard_map.110 = (bf16[128,1024]{1,0:T(8,128)(2,1)S(1)}, bf16[128,1024]{1,0:T(8,128)(2,1)S(1)}, bf16[128,1024]{1,0:T(8,128)(2,1)S(1)}, f32[16,1024]{1,0:T(8,128)S(1)}, f32[16,2048]{1,0:T(8,128)S(1)}) custom-call(bf16[128,1024]{1,0:T(8,128)(2,1)S(1)} %copy-done.1, bf16[128,1024]{1,0:T(8,128)(2,1)S(1)} %copy-done.2, bf16[128,1024]{1,0:T(8,128)(2,1)S(1)} %copy-done.3, ...), custom_call_target="tpu_custom_call" | custom-call | tf_op jit(solution)/shard_map/pallas_call | solution.py:578
  76.3 0.7 copy.17
  77.0 0.7 copy.18
  77.7 0.7 copy.19
  78.4 0.6 copy.20
  79.0 0.7 copy.21
Async XLA Ops:
  0.6 1.0 %copy-start = (bf16[128,2048]{1,0:T(8,128)(2,1)S(1)}, bf16[128,2048]{1,0:T(8,128)(2,1)}, u32[]{:S(2)}) copy-start(bf16[128,2048]{1,0:T(8,128)(2,1)} %refs_3_.1) | copy-start | bytes 1572868
  1.7 0.9 %copy-start.1 = (bf16[128,1024]{1,0:T(8,128)(2,1)S(1)}, bf16[128,1024]{1,0:T(8,128)(2,1)}, u32[]{:S(2)}) copy-start(bf16[128,1024]{1,0:T(8,128)(2,1)} %refs_0_.1) | copy-start | bytes 786436
  2.6 0.9 %copy-start.2 = (bf16[128,1024]{1,0:T(8,128)(2,1)S(1)}, bf16[128,1024]{1,0:T(8,128)(2,1)}, u32[]{:S(2)}) copy-start(bf16[128,1024]{1,0:T(8,128)(2,1)} %refs_1_.1) | copy-start | bytes 786436
  3.6 0.9 %copy-start.3 = (bf16[128,1024]{1,0:T(8,128)(2,1)S(1)}, bf16[128,1024]{1,0:T(8,128)(2,1)}, u32[]{:S(2)}) copy-start(bf16[128,1024]{1,0:T(8,128)(2,1)} %refs_2_.1) | copy-start | bytes 786436
  4.5 0.9 %copy-start.4 = (bf16[16,4096]{1,0:T(8,128)(2,1)S(1)}, bf16[16,4096]{1,0:T(8,128)(2,1)}, u32[]{:S(2)}) copy-start(bf16[16,4096]{1,0:T(8,128)(2,1)} %refs_6_.1) | copy-start | bytes 393220
  5.4 0.8 copy-start.5

commit v3 on v2

--- a/solution.py
+++ b/solution.py
@@ -164,6 +164,7 @@
 
 
 SCALE = HD ** (-0.5)
+LOG2E = 1.4426950408889634
 F32, BF16 = jnp.float32, jnp.bfloat16
 LOOK, DQ, DK, DV = range(4)
 
@@ -195,14 +196,15 @@
 
 def whole_kernel(
     n_seq,
-    q_ref, k_ref, v_ref, g_ref, w_ref, down_ref, up_ref,
+    q_ref, k_ref, v_ref, g_ref, w_ref, down_hbm, up_hbm,
     dq_ref, dk_ref, dv_ref, down_out, up_out,
-    g_all, w_all, queries, keys, values, douts, dout_send,
-    keys_t, values_t, probs, attn_send, dq_send, attn_full, dkeys, dvalues,
-    pair_send, pair_recv, pair_sum, upward, mid_mine, mid_theirs, pieces, gathered, totals,
+    down_ref, up_ref, g_all, w_all, queries, keys, values, douts, dout_send,
+    keys_t, values_t, probs, attn_send, dq_send, mid_send, mid_parts, up_all, dkeys, dvalues,
+    pair_send, pair_recv, pair_sum, upward, mid_mine, mid_theirs, down_mine, down_theirs,
+    down_all, pieces, sub_in, halves, gathered, totals, totals_away,
     local_sem, swap_send, swap_recv, in_send, in_recv, in_local, kv_send, kv_recv,
     do_send, do_recv, back_send, back_recv, back_local, pair_ssem, pair_rsem,
-    rs_send, rs_recv, ag_send, ag_recv,
+    rs_send, rs_recv, ag_send, ag_recv, up_send, up_recv, da_send, da_recv,
 ):
     me, head, sub = lax.axis_index("seq"), lax.axis_index("head"), lax.axis_index("sub")
     rank = down_ref.shape[0]
@@ -213,8 +215,11 @@
     first = head * (n_seq // 2)
     own_at = sub * HD
 
+    def step_of(n):
+        return 1 + lax.rem(n - 1 + sub * (n_seq // 2 - 1), n_seq - 1)
+
     def ring(n):
-        return lax.rem(me + n, n_seq)
+        return lax.rem(me + step_of(n), n_seq)
 
     def place_of(block):
         return lax.rem(block - first + n_seq, n_seq)
@@ -251,6 +256,10 @@
     own_w = pltpu.make_async_copy(w_ref, w_all.at[sub], local_sem.at[1])
     own_g.start()
     own_w.start()
+    own_down = pltpu.make_async_copy(down_hbm, down_ref, local_sem.at[2])
+    own_up = pltpu.make_async_copy(up_hbm, up_ref, local_sem.at[3])
+    own_down.start()
+    own_up.start()
     lax.fori_loop(1, peers, greet, 0)
     pl.semaphore_signal(
         barrier, inc=1, device_id={"head": 1 - head}, device_id_type=pl.DeviceIdType.MESH
@@ -294,8 +303,20 @@
 
     own_g.wait()
     own_w.wait()
+    own_down.wait()
+    own_up.wait()
     g_swap.wait()
     upward[...] = dot_nt(up_ref[:, :cols], g_all[0]) + dot_nt(up_ref[:, cols:], g_all[1])
+    up_all[o_me] = upward[...]
+
+    def up_copy(to, at):
+        return across(upward, up_all.at[at], up_send.at[to], up_recv.at[at], to)
+
+    def up_out_to(n, carry):
+        up_copy(ring(n), o_me).start()
+        return carry
+
+    lax.fori_loop(1, n_seq, up_out_to, 0)
     w_swap.wait()
     up_terms = three_terms(upward[...])
 
@@ -313,9 +334,6 @@
             dout_send.at[to], douts.at[own_rows(o_me), :], do_send.at[to], do_recv.at[me], to
         ).start()
         return carry
-
-    lax.fori_loop(1, n_seq, send_dout, 0)
-    douts[own_rows(o_me), :] = dout_of(me)
 
     for copy in own_in:
         copy.wait()
@@ -341,14 +359,19 @@
     kv_copy(1, o_me).start()
 
     def hand_on(n, carry):
-        frm = ring(n_seq - n)
+        frm = lax.rem(me - step_of(n) + n_seq, n_seq)
         for t in range(2):
             in_wait(t, frm).wait_recv()
             kv_copy(t, place_of(frm)).start()
         in_wait(2, frm).wait_recv()
         return carry
 
-    lax.fori_loop(1, n_seq, hand_on, 0)
+    def both(n, carry):
+        send_dout(n, carry)
+        return hand_on(n, carry)
+
+    lax.fori_loop(1, n_seq, both, 0)
+    douts[own_rows(o_me), :] = dout_of(me)
 
     def kv_arrived(order, carry):
         for t in range(2):
@@ -365,11 +388,14 @@
     keys_t[...] = keys[...].T
     values_t[...] = values[...].T
 
-    sinks = (attn_full, dq_ref, dk_ref, dv_ref)
+    sinks = (None, dq_ref, dk_ref, dv_ref)
+
+    def sink(kind, who):
+        return mid_parts.at[who] if kind == LOOK else sinks[kind].at[:, lanes(who)]
 
     def give(kind, src, order):
         to = lax.rem(order + first, n_seq)
-        dst = sinks[kind].at[:, lanes(me)]
+        dst = sink(kind, me)
 
         @pl.when(to == me)
         def _():
@@ -380,13 +406,13 @@
             across(src, dst, back_send.at[kind, to], back_recv.at[kind, me], to).start()
 
     def settle(kind):
-        src = attn_send.at[own_rows(0), :]
-        pltpu.make_async_copy(src, sinks[kind].at[:, lanes(me)], back_local.at[kind]).wait()
+        src = mid_send.at[0] if kind == LOOK else dq_send.at[own_rows(0), :]
+        pltpu.make_async_copy(src, sink(kind, me), back_local.at[kind]).wait()
 
         def one(n, carry):
             peer = ring(n)
             copy = across(
-                src, sinks[kind].at[:, lanes(peer)], back_send.at[kind, peer],
+                src, sink(kind, peer), back_send.at[kind, peer],
                 back_recv.at[kind, peer], peer,
             )
             copy.wait_send()
@@ -405,19 +431,22 @@
         base, extent = span(u)
         settled = extent - 2 * tile
         q = queries[u * tile : (u + 1) * tile, :]
-        scores = dot_nt(keys[:extent, :], q) * SCALE
+        scores = dot_nt(keys[:extent, :], q)
         key_at = lax.broadcasted_iota(jnp.int32, (2 * tile, tile), 0)
         row = lax.broadcasted_iota(jnp.int32, (2 * tile, tile), 1)
         query_at = row + jnp.where(row >= HD, HD, 0) + own_at
         edge = jnp.where(key_at <= query_at, scores[settled:, :], -jnp.inf)
         scores = edge if settled == 0 else jnp.concatenate((scores[:settled, :], edge), axis=0)
-        powers = jnp.exp(scores - jnp.max(scores, axis=0, keepdims=True))
+        powers = jnp.exp2((scores - jnp.max(scores, axis=0, keepdims=True)) * (SCALE * LOG2E))
         prob = powers * (1.0 / jnp.sum(powers, axis=0, keepdims=True))
         probs[base : base + extent, :] = prob
         attn = dot_nn(values_t[:, :extent], prob.astype(BF16)).T.astype(BF16)
         attn_send[u * tile : (u + 1) * tile, :] = attn
-        for order in (2 * u, 2 * u + 1):
-            give(LOOK, attn_send.at[order * HD : (order + 1) * HD, :], order)
+        middle = dot_nt(down_ref[:, lanes(me)], attn)
+        for part in range(2):
+            order = 2 * u + part
+            mid_send[order] = middle[:, part * HD : (part + 1) * HD]
+            give(LOOK, mid_send.at[order], order)
 
     def dout_arrived(n, carry):
         frm = ring(n)
@@ -443,74 +472,102 @@
             at = rows_of(order, sub)
             for t, total in enumerate((dkeys, dvalues)):
                 pair_sum[u, t, part] = (total[at, :] + pair_recv[u, t, part].astype(F32)).astype(BF16)
-                give(DK + t, pair_sum.at[u, t, part], order)
 
     mid_copy = remote(mid_mine, mid_theirs, swap_send.at[2], swap_recv.at[2], {"head": 1 - head})
+
+    down_copy = remote(down_mine, down_theirs, swap_send.at[3], swap_recv.at[3], {"sub": 1 - sub})
+    half_copy = remote(
+        pieces.at[pl.ds((1 - sub) * n_seq, n_seq)], sub_in, swap_send.at[4], swap_recv.at[4],
+        {"sub": 1 - sub},
+    )
+    away_copy = remote(totals, totals_away, swap_send.at[5], swap_recv.at[5], {"sub": 1 - sub})
 
     def lora_middle():
         settle(LOOK)
-        mid_mine[...] = dot_nt(down_ref[...], attn_full[...])
+        mid_mine[...] = jnp.sum(mid_parts[...], axis=0)
         mid_copy.start()
 
-    def peer_id(p):
-        return {"seq": p // 2, "sub": lax.rem(p, 2)}
+        def arrived(n, carry):
+            up_copy(ring(n), place_of(ring(n))).wait_send()
+            up_copy(ring(n), place_of(ring(n))).wait_recv()
+            return carry
+
+        lax.fori_loop(1, n_seq, arrived, 0)
+        upper = jnp.concatenate([up_all[order] for order in range(n_seq)], axis=1)
+        down_mine[...] = 2.0 * folded(dot_nn(three_terms(upper), attn_send[...]))
+        down_copy.start()
 
     def lora_parts():
         mid_copy.wait()
         middle = mid_mine[...] + mid_theirs[...]
         up_part = 2.0 * folded(dot_nn(three_terms(middle), g_all[head]))
-        down_part = 2.0 * folded(dot_nn(three_terms(upward[...]), attn_full[...]))
-        stack = jnp.concatenate((down_part, up_part[:, :feats], up_part[:, feats:]), axis=0)
-        half = stack.shape[0] // 2
-        for c in range(n_seq):
-            pieces[c] = stack[:half, c * HD : (c + 1) * HD]
-            pieces[n_seq + c] = stack[half:, c * HD : (c + 1) * HD]
-        gathered[mine] = pieces[mine]
+        for c in range(peers):
+            pieces[c] = up_part[:, c * HD : (c + 1) * HD]
+        half_copy.start()
+        down_copy.wait()
+        down_all[me] = down_mine[...] + down_theirs[...]
 
         def one(n, carry):
-            p = lax.rem(mine + n, peers)
-            remote(
-                pieces.at[p], gathered.at[mine], rs_send.at[p], rs_recv.at[mine], peer_id(p)
+            to = ring(n)
+            across(
+                down_all.at[me], down_all.at[me], da_send.at[to], da_recv.at[me], to
             ).start()
             return carry
 
-        lax.fori_loop(1, peers, one, 0)
+        lax.fori_loop(1, n_seq, one, 0)
+
+    def rs_copy(to, at):
+        return across(halves.at[to], gathered.at[at], rs_send.at[to], rs_recv.at[at], to)
+
+    def lora_spread():
+        half_copy.wait()
+        halves[...] = pieces[pl.ds(sub * n_seq, n_seq)] + sub_in[...]
+        gathered[me] = halves[me]
+
+        def one(n, carry):
+            rs_copy(ring(n), me).start()
+            return carry
+
+        lax.fori_loop(1, n_seq, one, 0)
+
+    def share_copy(to, at):
+        return across(totals.at[at], totals.at[at], ag_send.at[to], ag_recv.at[at], to)
 
     def lora_total():
         def one(n, carry):
-            p = lax.rem(mine + n, peers)
-            copy = remote(pieces.at[p], gathered.at[p], rs_send.at[p], rs_recv.at[p], peer_id(p))
-            copy.wait_send()
-            copy.wait_recv()
+            rs_copy(ring(n), ring(n)).wait_send()
+            rs_copy(ring(n), ring(n)).wait_recv()
             return carry
 
-        lax.fori_loop(1, peers, one, 0)
-        totals[mine] = jnp.sum(gathered[...], axis=0)
+        lax.fori_loop(1, n_seq, one, 0)
+        totals[me] = jnp.sum(gathered[...], axis=0)
 
         def share(n, carry):
-            p = lax.rem(mine + n, peers)
-            remote(
-                totals.at[mine], totals.at[mine], ag_send.at[p], ag_recv.at[mine], peer_id(p)
-            ).start()
+            share_copy(ring(n), me).start()
             return carry
 
-        lax.fori_loop(1, peers, share, 0)
+        lax.fori_loop(1, n_seq, share, 0)
 
     def lora_end():
         def one(n, carry):
-            p = lax.rem(mine + n, peers)
-            remote(totals.at[mine], totals.at[mine], ag_send.at[p], ag_recv.at[mine], peer_id(p)).wait_send()
-            remote(totals.at[p], totals.at[p], ag_send.at[p], ag_recv.at[p], peer_id(p)).wait_recv()
+            peer = ring(n)
+            share_copy(peer, me).wait_send()
+            share_copy(peer, peer).wait_recv()
+            across(down_all.at[me], down_all.at[me], da_send.at[peer], da_recv.at[me], peer).wait_send()
+            across(
+                down_all.at[peer], down_all.at[peer], da_send.at[peer], da_recv.at[peer], peer
+            ).wait_recv()
             return carry
 
-        lax.fori_loop(1, peers, one, 0)
-        over = rank // 2
+        lax.fori_loop(1, n_seq, one, 0)
+        away_copy.start()
+        away_copy.wait()
         for c in range(n_seq):
             at = slice(c * HD, (c + 1) * HD)
-            down_out[:, at] = totals[c, :rank, :]
-            up_out[:over, at] = totals[c, rank:, :]
-            up_out[over:, at] = totals[n_seq + c, :over, :]
-            up_out[:, feats + c * HD : feats + (c + 1) * HD] = totals[n_seq + c, over:, :]
+            down_out[:, at] = down_all[c]
+            here, away = totals[c], totals_away[c]
+            up_out[:, at] = jnp.where(sub == 0, here, away)
+            up_out[:, feats + c * HD : feats + (c + 1) * HD] = jnp.where(sub == 0, away, here)
 
     for u in reversed(range(tiles)):
         base, extent = span(u)
@@ -521,8 +578,6 @@
         delta = jnp.sum(prob * dprob, axis=0, keepdims=True)
         dscore = (prob * (dprob - delta) * SCALE).astype(BF16)
         dq_send[u * tile : (u + 1) * tile, :] = dot_nn(keys_t[:, :extent], dscore).T.astype(BF16)
-        for order in (2 * u, 2 * u + 1):
-            give(DQ, dq_send.at[order * HD : (order + 1) * HD, :], order)
         dk = dot_nn(dscore, q)
         dv = dot_nn(prob.astype(BF16), g)
         if u == tiles - 1:
@@ -542,8 +597,30 @@
             lora_middle()
         if u == tiles - 2:
             lora_parts()
+        if u == tiles - 3:
+            lora_spread()
+        if u == 0:
+            lora_total()
     pair_out(0)
-    lora_total()
+
+    def returned(kind, to):
+        order = place_of(to)
+        if kind == DQ:
+            return dq_send.at[own_rows(order), :]
+        return pair_sum.at[order // 2, kind - DK, lax.rem(order, 2)]
+
+    def give_back(n, carry):
+        to = ring(n)
+        for kind in (DQ, DK, DV):
+            across(
+                returned(kind, to), sink(kind, me), back_send.at[kind, to],
+                back_recv.at[kind, me], to,
+            ).start()
+        return carry
+
+    lax.fori_loop(1, n_seq, give_back, 0)
+    for kind in (DQ, DK, DV):
+        pltpu.make_async_copy(returned(kind, me), sink(kind, me), back_local.at[kind]).start()
 
     def in_sent(n, carry):
         for t in range(3):
@@ -571,17 +648,18 @@
     rank = adapter_up_weight.shape[0]
     total = 2 * n_seq * rows
     tiles = n_seq // 2
-    pieces = 3 * rank * feats // (2 * n_seq * HD)
     vmem = pl.BlockSpec(memory_space=pltpu.VMEM)
-    anywhere = pl.BlockSpec(memory_space=pl.ANY)
+    anywhere = pl.BlockSpec(memory_space=pltpu.HBM)
     dma = pltpu.SemaphoreType.DMA
     dq, dk, dv, down, up = pl.pallas_call(
         lambda *refs: whole_kernel(n_seq, *refs),
         out_shape=[jax.ShapeDtypeStruct((rows, feats), BF16)] * 3
         + [jax.ShapeDtypeStruct((rank, feats), F32), jax.ShapeDtypeStruct((rank, cols), F32)],
-        in_specs=[anywhere] * 5 + [vmem] * 2,
+        in_specs=[anywhere] * 7,
         out_specs=[anywhere] * 3 + [vmem] * 2,
         scratch_shapes=[
+            pltpu.VMEM((rank, feats), BF16),
+            pltpu.VMEM((rank, 2 * cols), BF16),
             pltpu.VMEM((2, rows, cols), BF16),
             pltpu.VMEM((2, feats, cols), BF16),
             pltpu.VMEM((total // 2, HD), BF16),
@@ -594,7 +672,9 @@
             pltpu.VMEM((tiles * (tiles + 1) * 2 * HD, 2 * HD), F32),
             pltpu.VMEM((total // 2, HD), BF16),
             pltpu.VMEM((total // 2, HD), BF16),
-            pltpu.VMEM((rows, feats), BF16),
+            pltpu.VMEM((n_seq, rank, rows), F32),
+            pltpu.VMEM((n_seq, rank, rows), F32),
+            pltpu.VMEM((n_seq, rank, rows), F32),
             pltpu.VMEM((total, HD), F32),
             pltpu.VMEM((total, HD), F32),
             pltpu.VMEM((tiles, 2, 2, rows, HD), BF16),
@@ -603,16 +683,23 @@
             pltpu.VMEM((rank, rows), F32),
             pltpu.VMEM((rank, rows), F32),
             pltpu.VMEM((rank, rows), F32),
-            pltpu.VMEM((2 * n_seq, pieces, HD), F32),
-            pltpu.VMEM((2 * n_seq, pieces, HD), F32),
-            pltpu.VMEM((2 * n_seq, pieces, HD), F32),
-            dma((2,)), dma((3,)), dma((3,)),
+            pltpu.VMEM((rank, HD), F32),
+            pltpu.VMEM((rank, HD), F32),
+            pltpu.VMEM((n_seq, rank, HD), F32),
+            pltpu.VMEM((2 * n_seq, rank, HD), F32),
+            pltpu.VMEM((n_seq, rank, HD), F32),
+            pltpu.VMEM((n_seq, rank, HD), F32),
+            pltpu.VMEM((n_seq, rank, HD), F32),
+            pltpu.VMEM((n_seq, rank, HD), F32),
+            pltpu.VMEM((n_seq, rank, HD), F32),
+            dma((4,)), dma((6,)), dma((6,)),
             dma((3, n_seq)), dma((3, n_seq)), dma((3,)),
             dma((2, n_seq)), dma((2, n_seq)),
             dma((n_seq,)), dma((n_seq,)),
             dma((4, n_seq)), dma((4, n_seq)), dma((4,)),
             dma((tiles,)), dma((tiles,)),
-            dma((2 * n_seq,)), dma((2 * n_seq,)), dma((2 * n_seq,)), dma((2 * n_seq,)),
+            dma((n_seq,)), dma((n_seq,)), dma((n_seq,)), dma((n_seq,)),
+            dma((n_seq,)), dma((n_seq,)), dma((n_seq,)), dma((n_seq,)),
         ],
         compiler_params=pltpu.CompilerParams(
             collective_id=0, has_side_effects=True, vmem_limit_bytes=48 * 1024 * 1024
@@ -635,6 +722,7 @@
         and feats == seq * HD
         and width == 2 * feats
         and lora == 16
+        and seq >= 6
     )
 
 

time: 80.4 us -> 78.6 us (0.978)
  Pallas kernels: 70.1 us -> 68.7 us
    pallas_call x1, Pallas kernels: 70.1 us -> 68.7 us  [on_device_heads(): pl.pallas_call(lambda *refs: whole_kernel(n_seq, *refs), out_shape=[jax.S...]
where the time goes in v3:
time: 78.6 us; the launch traced here: 78.2 us
  Pallas kernels  68.7 us (87%)
  local copies, waits for them, and re-layouts  8.94 us (11%)
    pallas_call x1, Pallas kernels, on_device_heads(): pl.pallas_call(lambda *refs: whole_kernel(n_seq, *refs), out_shape=[jax.S...  68.7 us
    unnamed x17, local copies, waits for them, and re-layouts  8.94 us

profile of v3, /device:TPU:1, one launch (start us, length us, event | category | flops | bytes accessed | tf_op | source)
XLA Modules:
  0.0 78.2 jit_solution(16863877641943928000)
XLA Ops:
  0.6 0.0 copy-start
  0.6 1.0 %copy-done = bf16[128,2048]{1,0:T(8,128)(2,1)S(1)} copy-done((bf16[128,2048]{1,0:T(8,128)(2,1)S(1)}, bf16[128,2048]{1,0:T(8,128)(2,1)}, u32[]{:S(2)}) %copy-start) | copy-done | bytes 524312
  1.7 0.0 copy-start.1
  1.7 0.9 %copy-done.1 = bf16[128,1024]{1,0:T(8,128)(2,1)S(1)} copy-done((bf16[128,1024]{1,0:T(8,128)(2,1)S(1)}, bf16[128,1024]{1,0:T(8,128)(2,1)}, u32[]{:S(2)}) %copy-start.1) | copy-done | bytes 262168
  2.6 0.0 copy-start.2
  2.6 0.9 %copy-done.2 = bf16[128,1024]{1,0:T(8,128)(2,1)S(1)} copy-done((bf16[128,1024]{1,0:T(8,128)(2,1)S(1)}, bf16[128,1024]{1,0:T(8,128)(2,1)}, u32[]{:S(2)}) %copy-start.2) | copy-done | bytes 262168
  3.6 0.0 copy-start.3
  3.6 0.9 %copy-done.3 = bf16[128,1024]{1,0:T(8,128)(2,1)S(1)} copy-done((bf16[128,1024]{1,0:T(8,128)(2,1)S(1)}, bf16[128,1024]{1,0:T(8,128)(2,1)}, u32[]{:S(2)}) %copy-start.3) | copy-done | bytes 262168
  4.5 0.0 copy-start.4
  4.5 0.9 %copy-done.4 = bf16[16,4096]{1,0:T(8,128)(2,1)S(1)} copy-done((bf16[16,4096]{1,0:T(8,128)(2,1)S(1)}, bf16[16,4096]{1,0:T(8,128)(2,1)}, u32[]{:S(2)}) %copy-start.4) | copy-done | bytes 131096
  5.4 0.0 copy-start.5
  5.4 0.8 copy-done.5
  6.2 68.7 %shard_map.110 = (bf16[128,1024]{1,0:T(8,128)(2,1)S(1)}, bf16[128,1024]{1,0:T(8,128)(2,1)S(1)}, bf16[128,1024]{1,0:T(8,128)(2,1)S(1)}, f32[16,1024]{1,0:T(8,128)S(1)}, f32[16,2048]{1,0:T(8,128)S(1)}) custom-call(bf16[128,1024]{1,0:T(8,128)(2,1)S(1)} %copy-done.1, bf16[128,1024]{1,0:T(8,128)(2,1)S(1)} %copy-done.2, bf16[128,1024]{1,0:T(8,128)(2,1)S(1)} %copy-done.3, ...), custom_call_target="tpu_custom_call" | custom-call | tf_op jit(solution)/shard_map/pallas_call | solution.py:654
  74.8 0.7 copy.17
  75.6 0.7 copy.18
  76.3 0.7 copy.19
  77.0 0.6 copy.20
  77.6 0.7 copy.21
Async XLA Ops:
  0.6 1.0 %copy-start = (bf16[128,2048]{1,0:T(8,128)(2,1)S(1)}, bf16[128,2048]{1,0:T(8,128)(2,1)}, u32[]{:S(2)}) copy-start(bf16[128,2048]{1,0:T(8,128)(2,1)} %refs_3_.1) | copy-start | bytes 1572868
  1.7 0.9 %copy-start.1 = (bf16[128,1024]{1,0:T(8,128)(2,1)S(1)}, bf16[128,1024]{1,0:T(8,128)(2,1)}, u32[]{:S(2)}) copy-start(bf16[128,1024]{1,0:T(8,128)(2,1)} %refs_0_.1) | copy-start | bytes 786436
  2.6 0.9 %copy-start.2 = (bf16[128,1024]{1,0:T(8,128)(2,1)S(1)}, bf16[128,1024]{1,0:T(8,128)(2,1)}, u32[]{:S(2)}) copy-start(bf16[128,1024]{1,0:T(8,128)(2,1)} %refs_1_.1) | copy-start | bytes 786436
  3.6 0.9 %copy-start.3 = (bf16[128,1024]{1,0:T(8,128)(2,1)S(1)}, bf16[128,1024]{1,0:T(8,128)(2,1)}, u32[]{:S(2)}) copy-start(bf16[128,1024]{1,0:T(8,128)(2,1)} %refs_2_.1) | copy-start | bytes 786436
  4.5 0.9 %copy-start.4 = (bf16[16,4096]{1,0:T(8,128)(2,1)S(1)}, bf16[16,4096]{1,0:T(8,128)(2,1)}, u32[]{:S(2)}) copy-start(bf16[16,4096]{1,0:T(8,128)(2,1)} %refs_6_.1) | copy-start | bytes 393220
  5.4 0.8 copy-start.5

commit v4 on v3

--- a/solution.py
+++ b/solution.py
@@ -601,17 +601,27 @@
             lora_spread()
         if u == 0:
             lora_total()
-    pair_out(0)
-
     def returned(kind, to):
         order = place_of(to)
         if kind == DQ:
             return dq_send.at[own_rows(order), :]
         return pair_sum.at[order // 2, kind - DK, lax.rem(order, 2)]
 
+    def give_queries(n, carry):
+        to = ring(n)
+        for kind in (DQ,):
+            across(
+                returned(kind, to), sink(kind, me), back_send.at[kind, to],
+                back_recv.at[kind, me], to,
+            ).start()
+        return carry
+
+    lax.fori_loop(1, n_seq, give_queries, 0)
+    pair_out(0)
+
     def give_back(n, carry):
         to = ring(n)
-        for kind in (DQ, DK, DV):
+        for kind in (DK, DV):
             across(
                 returned(kind, to), sink(kind, me), back_send.at[kind, to],
                 back_recv.at[kind, me], to,

time: 78.6 us -> 78.5 us (level)
  no operation moved by 1% of the time
where the time goes in v4:
time: 78.5 us; the launch traced here: 78.2 us
  Pallas kernels  68.6 us (87%)
  local copies, waits for them, and re-layouts  8.94 us (11%)
    pallas_call x1, Pallas kernels, on_device_heads(): pl.pallas_call(lambda *refs: whole_kernel(n_seq, *refs), out_shape=[jax.S...  68.6 us
    unnamed x17, local copies, waits for them, and re-layouts  8.94 us

profile of v4, /device:TPU:1, one launch (start us, length us, event | category | flops | bytes accessed | tf_op | source)
XLA Modules:
  0.0 78.2 jit_solution(15484859811453480062)
XLA Ops:
  0.6 0.0 copy-start
  0.6 1.0 %copy-done = bf16[128,2048]{1,0:T(8,128)(2,1)S(1)} copy-done((bf16[128,2048]{1,0:T(8,128)(2,1)S(1)}, bf16[128,2048]{1,0:T(8,128)(2,1)}, u32[]{:S(2)}) %copy-start) | copy-done | bytes 524312
  1.7 0.0 copy-start.1
  1.7 0.9 %copy-done.1 = bf16[128,1024]{1,0:T(8,128)(2,1)S(1)} copy-done((bf16[128,1024]{1,0:T(8,128)(2,1)S(1)}, bf16[128,1024]{1,0:T(8,128)(2,1)}, u32[]{:S(2)}) %copy-start.1) | copy-done | bytes 262168
  2.6 0.0 copy-start.2
  2.6 0.9 %copy-done.2 = bf16[128,1024]{1,0:T(8,128)(2,1)S(1)} copy-done((bf16[128,1024]{1,0:T(8,128)(2,1)S(1)}, bf16[128,1024]{1,0:T(8,128)(2,1)}, u32[]{:S(2)}) %copy-start.2) | copy-done | bytes 262168
  3.6 0.0 copy-start.3
  3.6 0.9 %copy-done.3 = bf16[128,1024]{1,0:T(8,128)(2,1)S(1)} copy-done((bf16[128,1024]{1,0:T(8,128)(2,1)S(1)}, bf16[128,1024]{1,0:T(8,128)(2,1)}, u32[]{:S(2)}) %copy-start.3) | copy-done | bytes 262168
  4.5 0.0 copy-start.4
  4.5 0.9 %copy-done.4 = bf16[16,4096]{1,0:T(8,128)(2,1)S(1)} copy-done((bf16[16,4096]{1,0:T(8,128)(2,1)S(1)}, bf16[16,4096]{1,0:T(8,128)(2,1)}, u32[]{:S(2)}) %copy-start.4) | copy-done | bytes 131096
  5.4 0.0 copy-start.5
  5.4 0.8 copy-done.5
  6.2 68.6 %shard_map.110 = (bf16[128,1024]{1,0:T(8,128)(2,1)S(1)}, bf16[128,1024]{1,0:T(8,128)(2,1)S(1)}, bf16[128,1024]{1,0:T(8,128)(2,1)S(1)}, f32[16,1024]{1,0:T(8,128)S(1)}, f32[16,2048]{1,0:T(8,128)S(1)}) custom-call(bf16[128,1024]{1,0:T(8,128)(2,1)S(1)} %copy-done.1, bf16[128,1024]{1,0:T(8,128)(2,1)S(1)} %copy-done.2, bf16[128,1024]{1,0:T(8,128)(2,1)S(1)} %copy-done.3, ...), custom_call_target="tpu_custom_call" | custom-call | tf_op jit(solution)/shard_map/pallas_call | solution.py:664
  74.8 0.7 copy.17
  75.5 0.7 copy.18
  76.2 0.7 copy.19
  76.9 0.6 copy.20
  77.6 0.7 copy.21
Async XLA Ops:
  0.6 1.0 %copy-start = (bf16[128,2048]{1,0:T(8,128)(2,1)S(1)}, bf16[128,2048]{1,0:T(8,128)(2,1)}, u32[]{:S(2)}) copy-start(bf16[128,2048]{1,0:T(8,128)(2,1)} %refs_3_.1) | copy-start | bytes 1572868
  1.7 0.9 %copy-start.1 = (bf16[128,1024]{1,0:T(8,128)(2,1)S(1)}, bf16[128,1024]{1,0:T(8,128)(2,1)}, u32[]{:S(2)}) copy-start(bf16[128,1024]{1,0:T(8,128)(2,1)} %refs_0_.1) | copy-start | bytes 786436
  2.6 0.9 %copy-start.2 = (bf16[128,1024]{1,0:T(8,128)(2,1)S(1)}, bf16[128,1024]{1,0:T(8,128)(2,1)}, u32[]{:S(2)}) copy-start(bf16[128,1024]{1,0:T(8,128)(2,1)} %refs_1_.1) | copy-start | bytes 786436
  3.6 0.9 %copy-start.3 = (bf16[128,1024]{1,0:T(8,128)(2,1)S(1)}, bf16[128,1024]{1,0:T(8,128)(2,1)}, u32[]{:S(2)}) copy-start(bf16[128,1024]{1,0:T(8,128)(2,1)} %refs_2_.1) | copy-start | bytes 786436
  4.5 0.9 %copy-start.4 = (bf16[16,4096]{1,0:T(8,128)(2,1)S(1)}, bf16[16,4096]{1,0:T(8,128)(2,1)}, u32[]{:S(2)}) copy-start(bf16[16,4096]{1,0:T(8,128)(2,1)} %refs_6_.1) | copy-start | bytes 393220
  5.4 0.8 copy-start.5
